TPU v7x, 32 devices: a whole 2x2x4 slice. The times are simulated.
32 devices in a mesh: row: 8 (over z, core), col: 4 (over y, x).
Axes of the slice: x: 2, y: 2, z: 4, core: 2. Of those that a mesh axis runs over, the one named last changes fastest.
Arguments:
- tokens: bfloat16 [16384, 1024], P(('row', 'col')), may hold values from -64 to 64, as said below
- merge_map: int32 [16384], P(('row', 'col')), may hold values from 0 to 511, as said below
- block_owner: int32 [32, 8], P(('row', 'col')), may hold values from -1 to 15, as said below
- neighbours: int32 [64, 4], P(('row', 'col')), may hold values from 0 to 7, as said below
- w_query: bfloat16 [1024, 512], replicated, may hold values from -0.1875 to 0.1875
- w_key: bfloat16 [1024, 512], replicated, may hold values from -0.1875 to 0.1875
- w_value: bfloat16 [1024, 512], replicated, may hold values from -0.1875 to 0.1875
Outputs:
- attended: bfloat16 [16384, 512], P(('row', 'col'))
Inputs may be any that keep to these rules, and one draw needn't show every extreme that they name: `merge_map`: within a tile, the slots of its live blocks (those whose block_owner is not -1) are each used by one or more tokens, and no other slot is used. `block_owner`: A tile's live blocks are its first ones, 1 to 8 of them, 8 in some tile of every column index; a code o names owned block o % 2 of the device with row index o // 2 and the tile's column index; within one column index every code is named exactly once; one tile names each row index at most once. `neighbours`: the entries of a row are distinct, and the first is the block's own candidate number. `tokens`: finite bfloat16 values.
All inputs are finite; a program needn't handle non-finite values.
Results may differ from a plain program's by a relative error of at most 0.019.
The roundings to bfloat16 on the way count: a program that leaves them out, or rounds other values in their place, can miss the bound.
Values may be sent and summed in bfloat16 or wider, within the bound.
No kernel may reach another device: no remote copies, remote signals or barrier semaphores. Data moves between devices by JAX's collectives and lax.ppermute only.
A program may use at most 64 MiB of HBM per device.

v0:
```python
import functools
import math

import jax
import jax.numpy as jnp
from jax import lax
from jax.experimental import pallas as pl
from jax.experimental.pallas import tpu as pltpu
from jax.sharding import PartitionSpec as P


HD = 64
BLK = 64
OWN = 2
LANES = 128
TAG = 8
STRIP = 8
RETURN_STEPS = 4


VMEM = pl.BlockSpec(memory_space=pltpu.VMEM)
SMEM = pl.BlockSpec(memory_space=pltpu.SMEM)
HBM = pl.BlockSpec(memory_space=pltpu.HBM)
PARAMS = pltpu.CompilerParams(vmem_limit_bytes=16 << 20)


def partner(i, k, n, back=False):
    if n & (n - 1) == 0:
        return i ^ k
    return (i - k + n) % n if back else (i + k) % n


def inner(i, k, n, back=False):
    m = n // 2
    side = (i >= m) * m
    return side + partner(i - side, k, m, back)


def across(i, n):
    m = n // 2
    return i + m - (i >= m) * n


def peer(i, k, n, back=False):
    m = n // 2
    return inner(i, k, n, back) if k < m else across(inner(i, k - m, n, back), n)


def order(n):
    return sorted(range(1, n), key=lambda k: (-(k.bit_length() - 1 if k > 1 else 0), k))


def rounds(x, axis, n, to):
    out = list(x)
    for k in order(len(x)):
        out[k] = lax.ppermute(x[k], axis, [(i, to(i, k, n)) for i in range(n)])
    return out


def cost(us):
    return pl.CostEstimate(
        flops=int(us * 8e8), bytes_accessed=int(us * 2e6), transcendentals=0
    )


FIRST = (0, BLK // 2)
SECOND = (BLK // 2, BLK - BLK // 2)
PARTS = (FIRST, SECOND)
HOME = ((0, BLK),)
MESSAGES = (
    ((True, *FIRST),),
    ((True, *SECOND),),
    ((False, *FIRST),),
    ((False, *SECOND),),
)


def slot_of(owner_ref, row, slots):
    slot = jnp.int32(-1)
    code = jnp.int32(-1)
    for b in range(slots):
        o = owner_ref[0, b]
        hit = (o >= 0) & (o // OWN == row)
        slot = jnp.where(hit, b, slot)
        code = jnp.where(hit, o % OWN, code)
    return slot, code


def rows_of(message):
    return sum(part[2] for part in message)


def merge_rows(hot, tok_ref, spots, pieces, ready):
    hot = hot.astype(jnp.float32)
    scale = 1.0 / jnp.maximum(jnp.sum(hot, axis=1, keepdims=True), 1.0)
    hot = hot.astype(jnp.bfloat16)
    for c in range(0, pieces, STRIP):
        ready(c // STRIP)
        columns = tok_ref[:, c * LANES : (c + STRIP) * LANES]
        sums = jnp.dot(hot, columns, preferred_element_type=jnp.float32)
        merged = (sums * scale).astype(jnp.bfloat16)
        row = 0
        for ref, rows in spots:
            for h in range(STRIP):
                at = (c + h) * rows
                ref[at : at + rows, :] = merged[row : row + rows, h * LANES : (h + 1) * LANES]
            row += rows


def first_merge_kernel(n, slots, tok_hbm, map_hbm, owner_hbm, *refs):
    m = n // 2
    outs = refs[:m]
    tok_ref, map_ref, ids_ref, code_ref, owner_ref, sems = refs[m:]
    _, width = tok_ref.shape
    pieces = width // LANES
    strips = [
        pltpu.make_async_copy(
            tok_hbm.at[:, c * LANES : (c + STRIP) * LANES],
            tok_ref.at[:, c * LANES : (c + STRIP) * LANES],
            sems.at[2 + c // STRIP],
        )
        for c in range(0, pieces, STRIP)
    ]
    get_owner = pltpu.make_async_copy(owner_hbm, owner_ref, sems.at[0])
    get_map = pltpu.make_async_copy(map_hbm, map_ref, sems.at[1])
    for copy in (get_owner, get_map, *strips):
        copy.start()
    me = lax.axis_index("row")
    get_owner.wait()
    to = [inner(me, k, n) for k in range(m)]
    near = [slot_of(owner_ref, to[k], slots) for k in range(m)]
    far = [slot_of(owner_ref, across(to[k], n), slots) for k in range(m)]

    def ids(slot, start, rows):
        base = jnp.where(slot >= 0, slot * BLK + start, -BLK)
        return lax.broadcasted_iota(jnp.int32, (rows, LANES), 0) + base

    (_, start, rows), pieces_rows = MESSAGES[0][0], pieces * MESSAGES[0][0][2]
    for k in range(m):
        outs[k][pieces_rows:, :] = jnp.full((TAG, LANES), far[k][1], jnp.int32).astype(
            jnp.bfloat16
        )
        code_ref[k * TAG : (k + 1) * TAG, :] = jnp.full(
            (TAG, LANES), near[k][1], jnp.int32
        ).astype(jnp.bfloat16)
    mine = jnp.concatenate([ids(far[k][0], start, rows)[:, :1] for k in range(m)], axis=0)
    get_map.wait()
    merge_rows(
        map_ref[...] == mine,
        tok_ref,
        [(outs[k], rows) for k in range(m)],
        pieces,
        lambda c: strips[c].wait(),
    )
    at = 0
    for message in MESSAGES[1:]:
        ((other, start, rows),) = message
        for k in range(m):
            ids_ref[at : at + rows, :] = ids((far if other else near)[k][0], start, rows)
            at += rows


def later_merge_kernel(m, tok_ref, map_ref, ids_ref, code_ref, *outs):
    pieces = tok_ref.shape[1] // LANES
    at = 0
    for i, message in enumerate(MESSAGES[1:]):
        ((other, start, rows),) = message
        hot = map_ref[...] == ids_ref[at : at + m * rows, :1]
        spots = [(outs[i * m + k], rows) for k in range(m)]
        merge_rows(hot, tok_ref, spots, pieces, lambda c: None)
        if start == 0:
            for k in range(m):
                outs[i * m + k][pieces * rows :, :] = code_ref[k * TAG : (k + 1) * TAG, :]
        at += m * rows


def pad(m):
    return -(-m // TAG) * TAG


def is_slot(tag, s):
    return tag[0:1, :].astype(jnp.float32) == float(s)


def masks_of(tags, rows):
    return [[jnp.broadcast_to(is_slot(tag, s), (rows, LANES)) for s in range(OWN)] for tag in tags]


def gather_kernel(m, rows, tagged, *refs):
    blocks = refs[:m]
    if tagged:
        (out_ref,) = refs[m:]
        size = out_ref.shape[0] - pad(m)
        for k in range(m):
            out_ref[size + k : size + k + 1, :] = blocks[k][size // OWN : size // OWN + 1, :]
        tags = [blocks[k][size // OWN : size // OWN + TAG, :] for k in range(m)]
    else:
        known_ref, out_ref = refs[m:]
        size = out_ref.shape[0]
        first = known_ref.shape[0] - pad(m)
        tags = [known_ref[first + k : first + k + 1, :] for k in range(m)]
    masks = masks_of(tags, rows)
    for h in range(0, size // OWN, rows):
        pick = [jnp.zeros((rows, LANES), jnp.bfloat16)] * OWN
        for k in range(m):
            block = blocks[k][h : h + rows, :]
            pick = [jnp.where(masks[k][s], block, pick[s]) for s in range(OWN)]
        for s in range(OWN):
            out_ref[s * (size // OWN) + h : s * (size // OWN) + h + rows, :] = pick[s]


def project_kernel(m, rows, tagged, wq_ref, wk_ref, wv_ref, cross_ref, *refs):
    blocks, refs = refs[:m], refs[m:]
    if tagged:
        q_ref, kv_ref, tag_ref, x_ref = refs
    else:
        tag_ref, q_ref, kv_ref, x_ref = refs
    pieces = x_ref.shape[1] // LANES
    size = pieces * rows
    if tagged:
        for k in range(m):
            tag_ref[k] = blocks[k][size : size + TAG, :]
    masks = masks_of([tag_ref[k] for k in range(m)], rows)
    for h in range(pieces):
        pick = [jnp.zeros((rows, LANES), jnp.bfloat16)] * OWN
        for k in range(m):
            block = blocks[k][h * rows : (h + 1) * rows, :]
            pick = [jnp.where(masks[k][s], block, pick[s]) for s in range(OWN)]
        for s in range(OWN):
            other = cross_ref[s * size + h * rows : s * size + (h + 1) * rows, :]
            x_ref[s * rows : (s + 1) * rows, h * LANES : (h + 1) * LANES] = pick[s] + other
    x = x_ref[...]
    width = wk_ref.shape[1]

    def mul(w):
        return jnp.dot(x, w[...], preferred_element_type=jnp.float32).astype(jnp.bfloat16)

    kv_ref[:, :width] = mul(wk_ref)
    kv_ref[:, width:] = mul(wv_ref)
    q_ref[...] = mul(wq_ref)


def attend_kernel(m, n_col, tag_ref, bias_ref, *refs):
    refs = list(refs)
    qs, refs = refs[: len(PARTS)], refs[len(PARTS) :]
    kvs, refs = refs[: len(PARTS) * n_col], refs[len(PARTS) * n_col :]
    outs, backs, (head_ref,) = refs[:m], refs[m : m + len(HOME)], refs[m + len(HOME) :]
    width = qs[0].shape[1]
    scale = 1.0 / math.sqrt(HD)
    low = lax.broadcasted_iota(jnp.int32, (BLK, LANES), 1) < HD
    zero = jnp.zeros((BLK, LANES), jnp.bfloat16)
    keys = bias_ref.shape[1]
    bias = jnp.concatenate(
        [jnp.broadcast_to(bias_ref[s : s + 1, :], (2 * BLK, keys)) for s in range(OWN)], axis=0
    )
    for h in range(0, width, LANES):
        rows = []
        for s in range(OWN):
            q = jnp.concatenate(
                [
                    qs[c][s * size : (s + 1) * size, h : h + LANES]
                    for c, (_, size) in enumerate(PARTS)
                ],
                axis=0,
            )
            rows += [jnp.where(low, q, zero), jnp.where(low, zero, q)]
        key = jnp.concatenate([kv[:, h : h + LANES] for kv in kvs], axis=0)
        value = jnp.concatenate([kv[:, width + h : width + h + LANES] for kv in kvs], axis=0)
        score = lax.dot_general(
            jnp.concatenate(rows, axis=0),
            key,
            (((1,), (1,)), ((), ())),
            preferred_element_type=jnp.float32,
        )
        score = score * scale + bias
        p = jnp.exp(score - jnp.max(score, axis=1, keepdims=True))
        total = jnp.sum(p, axis=1, keepdims=True)
        o = jnp.dot(p.astype(jnp.bfloat16), value, preferred_element_type=jnp.float32)
        o = (o * (1.0 / total)).astype(jnp.bfloat16)
        for s in range(OWN):
            at = 2 * s * BLK
            head_ref[s, :, h : h + LANES] = jnp.where(
                low, o[at : at + BLK], o[at + BLK : at + 2 * BLK]
            )
    for back, (start, rows) in zip(backs, HOME):
        for s in range(OWN):
            back[s * rows : (s + 1) * rows, :] = head_ref[s, start : start + rows, :]
    masks = masks_of([tag_ref[k] for k in range(m)], BLK)
    for k in range(m):
        for h in range(0, width, LANES):
            pick = zero
            for s in range(OWN):
                pick = jnp.where(masks[k][s], head_ref[s, :, h : h + LANES], pick)
            outs[k][:, h : h + LANES] = pick


def relay_kernel(m, known_ref, back_ref, *outs):
    rows, width = outs[0].shape
    first = known_ref.shape[0] - pad(m)
    masks = masks_of([known_ref[first + k : first + k + 1, :] for k in range(m)], rows)
    zero = jnp.zeros((rows, LANES), jnp.bfloat16)
    for k in range(m):
        for h in range(0, width, LANES):
            pick = zero
            for s in range(OWN):
                block = back_ref[s * rows : (s + 1) * rows, h : h + LANES]
                pick = jnp.where(masks[k][s], block, pick)
            outs[k][:, h : h + LANES] = pick


def spread_kernel(n, n_col, slots, map_ref, owner_ref, near_ref, out_ref, bias_ref):
    me = lax.axis_index("row")
    my_col = lax.axis_index("col")
    near = near_ref.shape[1]
    at = 0
    for _, rows in PARTS:
        for k in range(n_col):
            for t in range(OWN):
                cand = partner(my_col, k, n_col, True) * OWN + t
                for s in range(OWN):
                    hit = near_ref[s, 0] == cand
                    for j in range(1, near):
                        hit = hit | (near_ref[s, j] == cand)
                    bias_ref[s : s + 1, at : at + rows] = jnp.full(
                        (1, rows), jnp.where(hit, 0.0, -1e30), jnp.float32
                    )
                at += rows
    mm = map_ref[...]
    block = mm // BLK
    target = mm % BLK
    for k in range(n):
        slot, _ = slot_of(owner_ref, peer(me, k, n), slots)
        target = target + jnp.where((block == slot) & (slot >= 0), k * BLK, 0)
    toks = mm.shape[1]
    for k0 in range(0, n * BLK, LANES):
        ids = lax.broadcasted_iota(jnp.int32, (LANES, toks), 0) + k0
        hot = (ids == target).astype(jnp.float32)
        out_ref[:, k0 : k0 + LANES] = jnp.transpose(hot).astype(jnp.bfloat16)


def return_kernel(n, spread_ref, *refs):
    m = n // 2
    blocks, (out_hbm, all_ref, out_ref, sems) = refs[:-4], refs[-4:]
    for k in range(m):
        all_ref[k * BLK : (k + 1) * BLK, :] = blocks[k][...]
        for c, (start, rows) in enumerate(HOME):
            at = (m + k) * BLK + start
            all_ref[at : at + rows, :] = blocks[(1 + c) * m + k][...]
    step = out_ref.shape[0] // RETURN_STEPS
    copies = []
    for i in range(RETURN_STEPS):
        rows = slice(i * step, (i + 1) * step)
        out_ref[rows, :] = jnp.dot(
            spread_ref[rows, :], all_ref[...], preferred_element_type=jnp.float32
        ).astype(out_ref.dtype)
        copies.append(
            pltpu.make_async_copy(out_ref.at[rows, :], out_hbm.at[rows, :], sems.at[i])
        )
        copies[-1].start()
    for copy in copies:
        copy.wait()


def on_device(tokens, merge_map, block_owner, neighbours, w_query, w_key, w_value):
    n = lax.axis_size("row")
    n_col = lax.axis_size("col")
    toks, width = tokens.shape
    heads = w_query.shape[1]
    slots = block_owner.shape[1]
    bf16 = jnp.bfloat16

    def shape(*s, dtype=bf16):
        return jax.ShapeDtypeStruct(s, dtype)

    mm = pltpu.with_memory_space_constraint(merge_map.reshape(1, toks), pltpu.HBM)
    tokens = pltpu.with_memory_space_constraint(tokens, pltpu.HBM)
    block_owner = pltpu.with_memory_space_constraint(block_owner, pltpu.HBM)
    neighbours = pltpu.with_memory_space_constraint(neighbours, pltpu.HBM)
    m = n // 2
    pieces = width // LANES

    def message_shapes(message):
        size = rows_of(message) * pieces + TAG * any(part[1] == 0 for part in message)
        return [shape(size, LANES)] * m

    rest = sum(rows_of(message) for message in MESSAGES[1:]) * m
    *far0, toks_in, map_in, ids, codes = pl.pallas_call(
        functools.partial(first_merge_kernel, n, slots),
        out_shape=message_shapes(MESSAGES[0])
        + [
            shape(toks, width),
            shape(1, toks, dtype=jnp.int32),
            shape(rest, LANES, dtype=jnp.int32),
            shape(m * TAG, LANES),
        ],
        in_specs=[HBM] * 3,
        out_specs=[VMEM] * (m + 4),
        scratch_shapes=[
            pltpu.SMEM(block_owner.shape, jnp.int32),
            pltpu.SemaphoreType.DMA((2 + pieces // STRIP,)),
        ],
        compiler_params=PARAMS,
        cost_estimate=cost(2),
        name="merge",
    )(tokens, mm, block_owner)
    far0 = rounds(far0, "row", n, inner)
    outs = pl.pallas_call(
        functools.partial(later_merge_kernel, m),
        out_shape=[x for message in MESSAGES[1:] for x in message_shapes(message)],
        in_specs=[VMEM] * 4,
        out_specs=[VMEM] * (3 * m),
        compiler_params=PARAMS,
        cost_estimate=cost(2),
        name="merge_rest",
    )(toks_in, map_in, ids, codes)
    far1, own0, own1 = outs[:m], outs[m : 2 * m], outs[2 * m :]

    def gather(c, blocks, *known):
        rows = PARTS[c][1]
        out = pl.pallas_call(
            functools.partial(gather_kernel, m, rows, not known),
            out_shape=shape(OWN * rows * pieces + (0 if known else pad(m)), LANES),
            in_specs=[VMEM] * (m + len(known)),
            out_specs=VMEM,
            compiler_params=PARAMS,
            cost_estimate=cost(0.5),
            name="gather",
        )(*blocks, *known)
        return out, lax.ppermute(out, "row", [(i, across(i, n)) for i in range(n)])

    def project(c, cross, blocks, *tags):
        rows = PARTS[c][1]
        out = pl.pallas_call(
            functools.partial(project_kernel, m, rows, not tags),
            out_shape=[shape(OWN * rows, heads), shape(OWN * rows, 2 * heads)]
            + [shape(m, TAG, LANES)] * (not tags),
            in_specs=[VMEM] * (4 + m + len(tags)),
            out_specs=[VMEM] * (2 + (not tags)),
            scratch_shapes=[pltpu.VMEM((OWN * rows, width), bf16)],
            compiler_params=PARAMS,
            cost_estimate=cost(1),
            name="project",
        )(w_query, w_key, w_value, cross, *blocks, *tags)
        return out, rounds([out[1]] * n_col, "col", n_col, partner)

    far1 = rounds(far1, "row", n, inner)
    known, cross0 = gather(0, far0)
    own0 = rounds(own0, "row", n, inner)
    own1 = rounds(own1, "row", n, inner)
    _, cross1 = gather(1, far1, known)
    (q0, _, tags), kv0 = project(0, cross0, own0)
    (q1, _), kv1 = project(1, cross1, own1, tags)
    qs, kvs = [q0, q1], kv0 + kv1
    spread, bias = pl.pallas_call(
        functools.partial(spread_kernel, n, n_col, slots),
        out_shape=[
            shape(toks, n * BLK),
            shape(TAG, n_col * OWN * BLK, dtype=jnp.float32),
        ],
        in_specs=[VMEM, SMEM, SMEM],
        out_specs=[VMEM, VMEM],
        compiler_params=PARAMS,
        cost_estimate=cost(2),
        name="spread",
    )(map_in, block_owner, neighbours)
    outs = pl.pallas_call(
        functools.partial(attend_kernel, m, n_col),
        out_shape=[shape(BLK, heads)] * m + [shape(OWN * rows, heads) for _, rows in HOME],
        in_specs=[VMEM] * (2 + len(qs) + len(kvs)),
        out_specs=[VMEM] * (m + len(HOME)),
        scratch_shapes=[pltpu.VMEM((OWN, BLK, heads), bf16)],
        compiler_params=PARAMS,
        cost_estimate=cost(3),
        name="attend",
    )(tags, bias, *qs, *kvs)
    backs = [lax.ppermute(back, "row", [(i, across(i, n)) for i in range(n)]) for back in outs[m:]]
    to_sender = functools.partial(inner, back=True)
    returned = rounds(outs[:m], "row", n, to_sender)
    for c, (_, rows) in enumerate(HOME):
        relayed = pl.pallas_call(
            functools.partial(relay_kernel, m),
            out_shape=[shape(rows, heads)] * m,
            in_specs=[VMEM] * 2,
            out_specs=[VMEM] * m,
            compiler_params=PARAMS,
            cost_estimate=cost(0.5),
            name="relay",
        )(known, backs[c])
        returned += rounds(relayed, "row", n, to_sender)
    return pl.pallas_call(
        functools.partial(return_kernel, n),
        out_shape=shape(toks, heads),
        in_specs=[VMEM] * (1 + len(returned)),
        out_specs=HBM,
        scratch_shapes=[
            pltpu.VMEM((n * BLK, heads), bf16),
            pltpu.VMEM((toks, heads), bf16),
            pltpu.SemaphoreType.DMA((RETURN_STEPS,)),
        ],
        compiler_params=PARAMS,
        cost_estimate=cost(2),
        name="give_back",
    )(spread, *returned)


def solution(mesh):
    in_specs = (
        P(("row", "col"), None),
        P(("row", "col")),
        P(("row", "col"), None),
        P(("row", "col"), None),
        P(),
        P(),
        P(),
    )
    out_specs = P(("row", "col"), None)

    return jax.shard_map(
        on_device, mesh=mesh, in_specs=in_specs, out_specs=out_specs, check_vma=False
    )
```

profile of v0, /device:TPU:0, one launch (start us, length us, event | category | flops | bytes accessed | tf_op | source)
XLA Modules:
  0.0 57.7 jit_solution(7369691154229596560)
XLA Ops:
  0.0 1.6 %merge.1 = (bf16[264,128]{1,0:T(8,128)(2,1)S(1)}, bf16[264,128]{1,0:T(8,128)(2,1)S(1)}, bf16[264,128]{1,0:T(8,128)(2,1)S(1)}, bf16[264,128]{1,0:T(8,128)(2,1)S(1...) custom-call(bf16[512,1024]{1,0:T(8,128)(2,1)} %tok_hbm.1, ...), custom_call_target="tpu_custom_call" | custom-call | flops 1600000000 | bytes 4000000 | tf_op jit(solution)/shard_map/merge/pallas_call | solution.py:387
  1.6 0.6 collective-permute-start
  2.2 2.6 %collective-permute-start.1 = (bf16[264,128]{1,0:T(8,128)(2,1)S(1)}, bf16[264,128]{1,0:T(8,128)(2,1)S(1)}, u32[]{:S(2)}, u32[]{:S(2)}) collective-permute-start(bf16[264,128]{1,0:T(8,128)(2,1)S(1)} %get-tuple-element.45), channel_id=1, source_target_pairs={{0,8},{4,12},{8,0},{12,4},{16,24},{20,28},{24,16},{28,20},{1,9},{5... | collective-permute-start | bytes 202760 | tf_op jit(solution)/shard_map/ppermute | solution.py:56
  4.8 0.7 %merge_rest.1 = (bf16[256,128]{1,0:T(8,128)(2,1)S(1)}, bf16[256,128]{1,0:T(8,128)(2,1)S(1)}, bf16[256,128]{1,0:T(8,128)(2,1)S(1)}, bf16[256,128]{1,0:T(8,128)(2,...) custom-call(bf16[512,1024]{1,0:T(8,128)(2,1)S(1)} %get-tuple-element, ...), custom_call_target="tpu_custom_call" | custom-call | flops 1600000000 | bytes 4000000 | tf_op jit(solution)/shard_map/merge_rest/pallas_call | solution.py:407
  5.8 1.9 %collective-permute-start.8 = (bf16[256,128]{1,0:T(8,128)(2,1)S(1)}, bf16[256,128]{1,0:T(8,128)(2,1)S(1)}, u32[]{:S(2)}, u32[]{:S(2)}) collective-permute-start(bf16[256,128]{1,0:T(8,128)(2,1)S(1)} %get-tuple-element.59), channel_id=1, source_target_pairs={{0,8},{4,12},{8,0},{12,4},{16,24},{20,28},{24,16},{28,20},{1,9},{5... | collective-permute-start | bytes 196616 | tf_op jit(solution)/shard_map/ppermute | solution.py:56
  7.7 1.2 %collective-permute-done.2.refs_3_ = bf16[264,128]{1,0:T(8,128)(2,1)S(1)} collective-permute-done((bf16[264,128]{1,0:T(8,128)(2,1)S(1)}, bf16[264,128]{1,0:T(8,128)(2,1)S(1)}, u32[]{:S(2)}, u32[]{:S(2)}) %collective-permute-start.2) | collective-permute-done | bytes 67616 | tf_op jit(solution)/shard_map/ppermute | solution.py:56
  9.0 2.7 %collective-permute-start.3 = (bf16[520,128]{1,0:T(8,128)(2,1)S(1)}, bf16[520,128]{1,0:T(8,128)(2,1)S(1)}, u32[]{:S(2)}, u32[]{:S(2)}) collective-permute-start(bf16[520,128]{1,0:T(8,128)(2,1)S(1)} %gather.2.refs_4_.known_ref), channel_id=1, source_target_pairs={{0,16},{4,20},{8,24},{12,28},{16,0},{20,4},{24,8},{28,12},{1,17},{... | collective-permute-start | bytes 399368 | tf_op jit(solution)/shard_map/ppermute | solution.py:429
  11.8 1.4 %collective-permute-start.5 = (bf16[264,128]{1,0:T(8,128)(2,1)S(1)}, bf16[264,128]{1,0:T(8,128)(2,1)S(1)}, u32[]{:S(2)}, u32[]{:S(2)}) collective-permute-start(bf16[264,128]{1,0:T(8,128)(2,1)S(1)} %get-tuple-element.52), channel_id=1, source_target_pairs={{0,8},{4,12},{8,0},{12,4},{16,24},{20,28},{24,16},{28,20},{1,9},{5... | collective-permute-start | bytes 202760 | tf_op jit(solution)/shard_map/ppermute | solution.py:56
  13.5 1.2 %collective-permute-start.10 = (bf16[512,128]{1,0:T(8,128)(2,1)S(1)}, bf16[512,128]{1,0:T(8,128)(2,1)S(1)}, u32[]{:S(2)}, u32[]{:S(2)}) collective-permute-start(bf16[512,128]{1,0:T(8,128)(2,1)S(1)} %gather.3), channel_id=1, source_target_pairs={{0,16},{4,20},{8,24},{12,28},{16,0},{20,4},{24,8},{28,12},{1,17},{... | collective-permute-start | bytes 393224 | tf_op jit(solution)/shard_map/ppermute | solution.py:429
  14.8 0.5 collective-permute-start.11
  15.2 1.8 %collective-permute-done.5.refs_2_ = bf16[264,128]{1,0:T(8,128)(2,1)S(1)} collective-permute-done((bf16[264,128]{1,0:T(8,128)(2,1)S(1)}, bf16[264,128]{1,0:T(8,128)(2,1)S(1)}, u32[]{:S(2)}, u32[]{:S(2)}) %collective-permute-start.5) | collective-permute-done | bytes 67616 | tf_op jit(solution)/shard_map/ppermute | solution.py:56
  17.1 2.5 %collective-permute-start.12 = (bf16[256,128]{1,0:T(8,128)(2,1)S(1)}, bf16[256,128]{1,0:T(8,128)(2,1)S(1)}, u32[]{:S(2)}, u32[]{:S(2)}) collective-permute-start(bf16[256,128]{1,0:T(8,128)(2,1)S(1)} %get-tuple-element.63), channel_id=1, source_target_pairs={{0,8},{4,12},{8,0},{12,4},{16,24},{20,28},{24,16},{28,20},{1,9},{5... | collective-permute-start | bytes 196616 | tf_op jit(solution)/shard_map/ppermute | solution.py:56
  19.5 1.0 %collective-permute-done.6.refs_3_ = bf16[264,128]{1,0:T(8,128)(2,1)S(1)} collective-permute-done((bf16[264,128]{1,0:T(8,128)(2,1)S(1)}, bf16[264,128]{1,0:T(8,128)(2,1)S(1)}, u32[]{:S(2)}, u32[]{:S(2)}) %collective-permute-start.6) | collective-permute-done | bytes 67616 | tf_op jit(solution)/shard_map/ppermute | solution.py:56
  20.7 0.7 %project.2 = (bf16[64,512]{1,0:T(8,128)(2,1)S(1)}, bf16[64,1024]{1,0:T(8,128)(2,1)S(1)}, bf16[4,8,128]{2,1,0:T(8,128)(2,1)S(1)}) custom-call(bf16[1024,512]{1,0:T(8,128)(2,1)S(1)} %copy-done, bf16[1024,512]{1,0:T(8,128)(2,1)S(1)} %copy-done.1, bf16[1024,512]{1,0:T(8,128)(2,1)S(1)} %copy-done.2, bf16[520,128]{1,0:T(8,128)(2,1)S(1)} %collective-permute-done.3.cross_ref, ...), custom_call_target="tpu_custom_call" | custom-call | flops 800000000 | bytes 2000000 | tf_op jit(solution)/shard_map/project/pallas_call | solution.py:433
  21.4 1.3 %collective-permute-done.12.refs_2_ = bf16[256,128]{1,0:T(8,128)(2,1)S(1)} collective-permute-done((bf16[256,128]{1,0:T(8,128)(2,1)S(1)}, bf16[256,128]{1,0:T(8,128)(2,1)S(1)}, u32[]{:S(2)}, u32[]{:S(2)}) %collective-permute-start.12) | collective-permute-done | bytes 65568 | tf_op jit(solution)/shard_map/ppermute | solution.py:56
  22.8 3.0 %collective-permute-done.13.refs_3_ = bf16[256,128]{1,0:T(8,128)(2,1)S(1)} collective-permute-done((bf16[256,128]{1,0:T(8,128)(2,1)S(1)}, bf16[256,128]{1,0:T(8,128)(2,1)S(1)}, u32[]{:S(2)}, u32[]{:S(2)}) %collective-permute-start.13) | collective-permute-done | bytes 65568 | tf_op jit(solution)/shard_map/ppermute | solution.py:56
  25.8 0.7 %project.3 = (bf16[64,512]{1,0:T(8,128)(2,1)S(1)}, bf16[64,1024]{1,0:T(8,128)(2,1)S(1)}) custom-call(bf16[1024,512]{1,0:T(8,128)(2,1)S(1)} %copy-done, bf16[1024,512]{1,0:T(8,128)(2,1)S(1)} %copy-done.1, bf16[1024,512]{1,0:T(8,128)(2,1)S(1)} %copy-done.2, bf16[512,128]{1,0:T(8,128)(2,1)S(1)} %collective-permute-done.10.cross_ref, ...), custom_call_target="tpu_custom_call" | custom-call | flops 800000000 | bytes 2000000 | tf_op jit(solution)/shard_map/project/pallas_call | solution.py:433
  26.4 1.6 %collective-permute-start.17 = (bf16[64,1024]{1,0:T(8,128)(2,1)S(1)}, bf16[64,1024]{1,0:T(8,128)(2,1)S(1)}, u32[]{:S(2)}, u32[]{:S(2)}) collective-permute-start(bf16[64,1024]{1,0:T(8,128)(2,1)S(1)} %get-tuple-element.67.refs_6_), channel_id=1, source_target_pairs={{0,1},{1,0},{2,3},{3,2},{4,5},{5,4},{6,7},{7,6},{8,9},{9,8},{10,11... | collective-permute-start | bytes 393224 | tf_op jit(solution)/shard_map/ppermute | solution.py:56
  28.0 1.5 %collective-permute-start.18 = (bf16[64,1024]{1,0:T(8,128)(2,1)S(1)}, bf16[64,1024]{1,0:T(8,128)(2,1)S(1)}, u32[]{:S(2)}, u32[]{:S(2)}) collective-permute-start(bf16[64,1024]{1,0:T(8,128)(2,1)S(1)} %get-tuple-element.67.refs_6_), channel_id=1, source_target_pairs={{0,2},{1,3},{2,0},{3,1},{4,6},{5,7},{6,4},{7,5},{8,10},{9,11},{10,... | collective-permute-start | bytes 393224 | tf_op jit(solution)/shard_map/ppermute | solution.py:56
  29.5 0.5 collective-permute-start.19
  30.0 1.5 %collective-permute-start.14 = (bf16[64,1024]{1,0:T(8,128)(2,1)S(1)}, bf16[64,1024]{1,0:T(8,128)(2,1)S(1)}, u32[]{:S(2)}, u32[]{:S(2)}) collective-permute-start(bf16[64,1024]{1,0:T(8,128)(2,1)S(1)} %get-tuple-element.66.refs_2_), channel_id=1, source_target_pairs={{0,1},{1,0},{2,3},{3,2},{4,5},{5,4},{6,7},{7,6},{8,9},{9,8},{10,11... | collective-permute-start | bytes 393224 | tf_op jit(solution)/shard_map/ppermute | solution.py:56
  31.5 1.5 %collective-permute-start.15 = (bf16[64,1024]{1,0:T(8,128)(2,1)S(1)}, bf16[64,1024]{1,0:T(8,128)(2,1)S(1)}, u32[]{:S(2)}, u32[]{:S(2)}) collective-permute-start(bf16[64,1024]{1,0:T(8,128)(2,1)S(1)} %get-tuple-element.66.refs_2_), channel_id=1, source_target_pairs={{0,2},{1,3},{2,0},{3,1},{4,6},{5,7},{6,4},{7,5},{8,10},{9,11},{10,... | collective-permute-start | bytes 393224 | tf_op jit(solution)/shard_map/ppermute | solution.py:56
  33.0 2.3 %collective-permute-start.16 = (bf16[64,1024]{1,0:T(8,128)(2,1)S(1)}, bf16[64,1024]{1,0:T(8,128)(2,1)S(1)}, u32[]{:S(2)}, u32[]{:S(2)}) collective-permute-start(bf16[64,1024]{1,0:T(8,128)(2,1)S(1)} %get-tuple-element.66.refs_2_), channel_id=1, source_target_pairs={{0,3},{1,2},{2,1},{3,0},{4,7},{5,6},{6,5},{7,4},{8,11},{9,10},{10,... | collective-permute-start | bytes 393224 | tf_op jit(solution)/shard_map/ppermute | solution.py:56
  35.3 1.1 %spread.1 = (bf16[512,512]{1,0:T(8,128)(2,1)S(1)}, f32[8,512]{1,0:T(8,128)S(1)}) custom-call(s32[1,512]{1,0:T(1,128)S(1)} %get-tuple-element.41.map_ref, s32[1,8]{1,0:T(1,128)} %owner_ref.1, s32[2,4]{1,0:T(2,128)} %near_ref.1), custom_call_target="tpu_custom_call" | custom-call | flops 1600000000 | bytes 4000000 | tf_op jit(solution)/shard_map/spread/pallas_call | solution.py:454
  36.8 1.9 %collective-permute-done.14.refs_3_ = bf16[64,1024]{1,0:T(8,128)(2,1)S(1)} collective-permute-done((bf16[64,1024]{1,0:T(8,128)(2,1)S(1)}, bf16[64,1024]{1,0:T(8,128)(2,1)S(1)}, u32[]{:S(2)}, u32[]{:S(2)}) %collective-permute-start.14) | collective-permute-done | bytes 131104 | tf_op jit(solution)/shard_map/ppermute | solution.py:56
  38.7 3.0 %collective-permute-done.15.refs_4_ = bf16[64,1024]{1,0:T(8,128)(2,1)S(1)} collective-permute-done((bf16[64,1024]{1,0:T(8,128)(2,1)S(1)}, bf16[64,1024]{1,0:T(8,128)(2,1)S(1)}, u32[]{:S(2)}, u32[]{:S(2)}) %collective-permute-start.15) | collective-permute-done | bytes 131104 | tf_op jit(solution)/shard_map/ppermute | solution.py:56
  41.7 1.4 %attend.1 = (bf16[64,512]{1,0:T(8,128)(2,1)S(1)}, bf16[64,512]{1,0:T(8,128)(2,1)S(1)}, bf16[64,512]{1,0:T(8,128)(2,1)S(1)}, bf16[64,512]{1,0:T(8,128)(2,1)S(1)}, bf16[128,512]{1,0:T(8,128)(2,1)S(1)}) custom-call(bf16[4,8,128]{2,1,0:T(8,128)(2,1)S(1)} %get-tuple-element.54.refs_4_.tag_ref, f32[8,512]{1,0:T(8,128)S(1)} %get-tuple-element.55.bias_ref, ...), custom_call_target="tpu_custom_call" | custom-call | flops 2400000000 | bytes 6000000 | tf_op jit(solution)/shard_map/attend/pallas_call | solution.py:466
  43.5 2.1 %collective-permute-start.21 = (bf16[64,512]{1,0:T(8,128)(2,1)S(1)}, bf16[64,512]{1,0:T(8,128)(2,1)S(1)}, u32[]{:S(2)}, u32[]{:S(2)}) collective-permute-start(bf16[64,512]{1,0:T(8,128)(2,1)S(1)} %get-tuple-element.70), channel_id=1, source_target_pairs={{0,8},{4,12},{8,0},{12,4},{16,24},{20,28},{24,16},{28,20},{1,9},{5... | collective-permute-start | bytes 196616 | tf_op jit(solution)/shard_map/ppermute | solution.py:56
  45.7 5.3 %collective-permute-done.23.back_ref = bf16[128,512]{1,0:T(8,128)(2,1)S(1)} collective-permute-done((bf16[128,512]{1,0:T(8,128)(2,1)S(1)}, bf16[128,512]{1,0:T(8,128)(2,1)S(1)}, u32[]{:S(2)}, u32[]{:S(2)}) %collective-permute-start.23) | collective-permute-done | bytes 131104 | tf_op jit(solution)/shard_map/ppermute | solution.py:476
  51.2 1.8 %collective-permute-start.26 = (bf16[64,512]{1,0:T(8,128)(2,1)S(1)}, bf16[64,512]{1,0:T(8,128)(2,1)S(1)}, u32[]{:S(2)}, u32[]{:S(2)}) collective-permute-start(bf16[64,512]{1,0:T(8,128)(2,1)S(1)} %get-tuple-element.76), channel_id=1, source_target_pairs={{0,12},{4,8},{8,4},{12,0},{16,28},{20,24},{24,20},{28,16},{1,13},{... | collective-permute-start | bytes 196616 | tf_op jit(solution)/shard_map/ppermute | solution.py:56
  53.0 3.2 %collective-permute-done.25.refs_6_ = bf16[64,512]{1,0:T(8,128)(2,1)S(1)} collective-permute-done((bf16[64,512]{1,0:T(8,128)(2,1)S(1)}, bf16[64,512]{1,0:T(8,128)(2,1)S(1)}, u32[]{:S(2)}, u32[]{:S(2)}) %collective-permute-start.25) | collective-permute-done | bytes 65568 | tf_op jit(solution)/shard_map/ppermute | solution.py:56
  56.5 1.1 %give_back.1 = bf16[512,512]{1,0:T(8,128)(2,1)} custom-call(bf16[512,512]{1,0:T(8,128)(2,1)S(1)} %get-tuple-element.42.spread_ref, bf16[64,512]{1,0:T(8,128)(2,1)S(1)} %get-tuple-element.68.refs_0_, bf16[64,512]{1,0:T(8,128)(2,1)S(1)} %collective-permute-done.20.refs_1_, bf16[64,512]{1,0:T(8,128)(2,1)S(1)} %collective-permute-done.21.refs_2_, ...), custom_call_target="tpu_custom_call" | custom-call | flops 1600000000 | bytes 4000000 | tf_op jit(solution)/shard_map/give_back/pallas_call | solution.py:490
  (38 shorter events, 2.5 us)
Async XLA Ops:
  1.6 6.1 %collective-permute-start = (bf16[264,128]{1,0:T(8,128)(2,1)S(1)}, bf16[264,128]{1,0:T(8,128)(2,1)S(1)}, u32[]{:S(2)}, u32[]{:S(2)}) collective-permute-start(bf16[264,128]{1,0:T(8,128)(2,1)S(1)} %get-tuple-element.44), channel_id=1, source_target_pairs={{0,4},{4,0},{8,12},{12,8},{16,20},{20,16},{24,28},{28,24},{1,5},{5... | collective-permute-start | bytes 202760 | tf_op jit(solution)/shard_map/ppermute | solution.py:56
  2.2 5.6 %collective-permute-start.1 = (bf16[264,128]{1,0:T(8,128)(2,1)S(1)}, bf16[264,128]{1,0:T(8,128)(2,1)S(1)}, u32[]{:S(2)}, u32[]{:S(2)}) collective-permute-start(bf16[264,128]{1,0:T(8,128)(2,1)S(1)} %get-tuple-element.45), channel_id=1, source_target_pairs={{0,8},{4,12},{8,0},{12,4},{16,24},{20,28},{24,16},{28,20},{1,9},{5... | collective-permute-start | bytes 202760 | tf_op jit(solution)/shard_map/ppermute | solution.py:56
  4.8 4.1 %collective-permute-start.2 = (bf16[264,128]{1,0:T(8,128)(2,1)S(1)}, bf16[264,128]{1,0:T(8,128)(2,1)S(1)}, u32[]{:S(2)}, u32[]{:S(2)}) collective-permute-start(bf16[264,128]{1,0:T(8,128)(2,1)S(1)} %get-tuple-element.46), channel_id=1, source_target_pairs={{0,12},{4,8},{8,4},{12,0},{16,28},{20,24},{24,20},{28,16},{1,13},{... | collective-permute-start | bytes 202760 | tf_op jit(solution)/shard_map/ppermute | solution.py:56
  4.8 15.9 %copy-start.2 = (bf16[1024,512]{1,0:T(8,128)(2,1)S(1)}, bf16[1024,512]{1,0:T(8,128)(2,1)}, u32[]{:S(2)}) copy-start(bf16[1024,512]{1,0:T(8,128)(2,1)} %wv_ref.3) | copy-start | bytes 3145732
  5.5 6.3 %collective-permute-start.7 = (bf16[256,128]{1,0:T(8,128)(2,1)S(1)}, bf16[256,128]{1,0:T(8,128)(2,1)S(1)}, u32[]{:S(2)}, u32[]{:S(2)}) collective-permute-start(bf16[256,128]{1,0:T(8,128)(2,1)S(1)} %get-tuple-element.58), channel_id=1, source_target_pairs={{0,4},{4,0},{8,12},{12,8},{16,20},{20,16},{24,28},{28,24},{1,5},{5... | collective-permute-start | bytes 196616 | tf_op jit(solution)/shard_map/ppermute | solution.py:56
  5.8 7.5 %collective-permute-start.8 = (bf16[256,128]{1,0:T(8,128)(2,1)S(1)}, bf16[256,128]{1,0:T(8,128)(2,1)S(1)}, u32[]{:S(2)}, u32[]{:S(2)}) collective-permute-start(bf16[256,128]{1,0:T(8,128)(2,1)S(1)} %get-tuple-element.59), channel_id=1, source_target_pairs={{0,8},{4,12},{8,0},{12,4},{16,24},{20,28},{24,16},{28,20},{1,9},{5... | collective-permute-start | bytes 196616 | tf_op jit(solution)/shard_map/ppermute | solution.py:56
  7.7 5.8 %collective-permute-start.9 = (bf16[256,128]{1,0:T(8,128)(2,1)S(1)}, bf16[256,128]{1,0:T(8,128)(2,1)S(1)}, u32[]{:S(2)}, u32[]{:S(2)}) collective-permute-start(bf16[256,128]{1,0:T(8,128)(2,1)S(1)} %get-tuple-element.60), channel_id=1, source_target_pairs={{0,12},{4,8},{8,4},{12,0},{16,28},{20,24},{24,20},{28,16},{1,13},{... | collective-permute-start | bytes 196616 | tf_op jit(solution)/shard_map/ppermute | solution.py:56
  8.9 11.8 %copy-start.1 = (bf16[1024,512]{1,0:T(8,128)(2,1)S(1)}, bf16[1024,512]{1,0:T(8,128)(2,1)}, u32[]{:S(2)}) copy-start(bf16[1024,512]{1,0:T(8,128)(2,1)} %wk_ref.3) | copy-start | bytes 3145732
  9.0 11.8 %copy-start = (bf16[1024,512]{1,0:T(8,128)(2,1)S(1)}, bf16[1024,512]{1,0:T(8,128)(2,1)}, u32[]{:S(2)}) copy-start(bf16[1024,512]{1,0:T(8,128)(2,1)} %wq_ref.3) | copy-start | bytes 3145732
  9.0 11.7 %collective-permute-start.3 = (bf16[520,128]{1,0:T(8,128)(2,1)S(1)}, bf16[520,128]{1,0:T(8,128)(2,1)S(1)}, u32[]{:S(2)}, u32[]{:S(2)}) collective-permute-start(bf16[520,128]{1,0:T(8,128)(2,1)S(1)} %gather.2.refs_4_.known_ref), channel_id=1, source_target_pairs={{0,16},{4,20},{8,24},{12,28},{16,0},{20,4},{24,8},{28,12},{1,17},{... | collective-permute-start | bytes 399368 | tf_op jit(solution)/shard_map/ppermute | solution.py:429
  11.6 3.1 %collective-permute-start.4 = (bf16[264,128]{1,0:T(8,128)(2,1)S(1)}, bf16[264,128]{1,0:T(8,128)(2,1)S(1)}, u32[]{:S(2)}, u32[]{:S(2)}) collective-permute-start(bf16[264,128]{1,0:T(8,128)(2,1)S(1)} %get-tuple-element.51), channel_id=1, source_target_pairs={{0,4},{4,0},{8,12},{12,8},{16,20},{20,16},{24,28},{28,24},{1,5},{5... | collective-permute-start | bytes 202760 | tf_op jit(solution)/shard_map/ppermute | solution.py:56
  11.8 5.2 %collective-permute-start.5 = (bf16[264,128]{1,0:T(8,128)(2,1)S(1)}, bf16[264,128]{1,0:T(8,128)(2,1)S(1)}, u32[]{:S(2)}, u32[]{:S(2)}) collective-permute-start(bf16[264,128]{1,0:T(8,128)(2,1)S(1)} %get-tuple-element.52), channel_id=1, source_target_pairs={{0,8},{4,12},{8,0},{12,4},{16,24},{20,28},{24,16},{28,20},{1,9},{5... | collective-permute-start | bytes 202760 | tf_op jit(solution)/shard_map/ppermute | solution.py:56
  13.2 7.3 %collective-permute-start.6 = (bf16[264,128]{1,0:T(8,128)(2,1)S(1)}, bf16[264,128]{1,0:T(8,128)(2,1)S(1)}, u32[]{:S(2)}, u32[]{:S(2)}) collective-permute-start(bf16[264,128]{1,0:T(8,128)(2,1)S(1)} %get-tuple-element.53), channel_id=1, source_target_pairs={{0,12},{4,8},{8,4},{12,0},{16,28},{20,24},{24,20},{28,16},{1,13},{... | collective-permute-start | bytes 202760 | tf_op jit(solution)/shard_map/ppermute | solution.py:56
  13.5 12.2 %collective-permute-start.10 = (bf16[512,128]{1,0:T(8,128)(2,1)S(1)}, bf16[512,128]{1,0:T(8,128)(2,1)S(1)}, u32[]{:S(2)}, u32[]{:S(2)}) collective-permute-start(bf16[512,128]{1,0:T(8,128)(2,1)S(1)} %gather.3), channel_id=1, source_target_pairs={{0,16},{4,20},{8,24},{12,28},{16,0},{20,4},{24,8},{28,12},{1,17},{... | collective-permute-start | bytes 393224 | tf_op jit(solution)/shard_map/ppermute | solution.py:429
  14.8 6.6 %collective-permute-start.11 = (bf16[256,128]{1,0:T(8,128)(2,1)S(1)}, bf16[256,128]{1,0:T(8,128)(2,1)S(1)}, u32[]{:S(2)}, u32[]{:S(2)}) collective-permute-start(bf16[256,128]{1,0:T(8,128)(2,1)S(1)} %get-tuple-element.62), channel_id=1, source_target_pairs={{0,4},{4,0},{8,12},{12,8},{16,20},{20,16},{24,28},{28,24},{1,5},{5... | collective-permute-start | bytes 196616 | tf_op jit(solution)/shard_map/ppermute | solution.py:56
  17.1 5.7 %collective-permute-start.12 = (bf16[256,128]{1,0:T(8,128)(2,1)S(1)}, bf16[256,128]{1,0:T(8,128)(2,1)S(1)}, u32[]{:S(2)}, u32[]{:S(2)}) collective-permute-start(bf16[256,128]{1,0:T(8,128)(2,1)S(1)} %get-tuple-element.63), channel_id=1, source_target_pairs={{0,8},{4,12},{8,0},{12,4},{16,24},{20,28},{24,16},{28,20},{1,9},{5... | collective-permute-start | bytes 196616 | tf_op jit(solution)/shard_map/ppermute | solution.py:56
  20.5 5.2 %collective-permute-start.13 = (bf16[256,128]{1,0:T(8,128)(2,1)S(1)}, bf16[256,128]{1,0:T(8,128)(2,1)S(1)}, u32[]{:S(2)}, u32[]{:S(2)}) collective-permute-start(bf16[256,128]{1,0:T(8,128)(2,1)S(1)} %get-tuple-element.64), channel_id=1, source_target_pairs={{0,12},{4,8},{8,4},{12,0},{16,28},{20,24},{24,20},{28,16},{1,13},{... | collective-permute-start | bytes 196616 | tf_op jit(solution)/shard_map/ppermute | solution.py:56
  26.4 6.6 %collective-permute-start.17 = (bf16[64,1024]{1,0:T(8,128)(2,1)S(1)}, bf16[64,1024]{1,0:T(8,128)(2,1)S(1)}, u32[]{:S(2)}, u32[]{:S(2)}) collective-permute-start(bf16[64,1024]{1,0:T(8,128)(2,1)S(1)} %get-tuple-element.67.refs_6_), channel_id=1, source_target_pairs={{0,1},{1,0},{2,3},{3,2},{4,5},{5,4},{6,7},{7,6},{8,9},{9,8},{10,11... | collective-permute-start | bytes 393224 | tf_op jit(solution)/shard_map/ppermute | solution.py:56
  28.0 8.4 %collective-permute-start.18 = (bf16[64,1024]{1,0:T(8,128)(2,1)S(1)}, bf16[64,1024]{1,0:T(8,128)(2,1)S(1)}, u32[]{:S(2)}, u32[]{:S(2)}) collective-permute-start(bf16[64,1024]{1,0:T(8,128)(2,1)S(1)} %get-tuple-element.67.refs_6_), channel_id=1, source_target_pairs={{0,2},{1,3},{2,0},{3,1},{4,6},{5,7},{6,4},{7,5},{8,10},{9,11},{10,... | collective-permute-start | bytes 393224 | tf_op jit(solution)/shard_map/ppermute | solution.py:56
  29.5 7.3 %collective-permute-start.19 = (bf16[64,1024]{1,0:T(8,128)(2,1)S(1)}, bf16[64,1024]{1,0:T(8,128)(2,1)S(1)}, u32[]{:S(2)}, u32[]{:S(2)}) collective-permute-start(bf16[64,1024]{1,0:T(8,128)(2,1)S(1)} %get-tuple-element.67.refs_6_), channel_id=1, source_target_pairs={{0,3},{1,2},{2,1},{3,0},{4,7},{5,6},{6,5},{7,4},{8,11},{9,10},{10,... | collective-permute-start | bytes 393224 | tf_op jit(solution)/shard_map/ppermute | solution.py:56
  30.0 8.7 %collective-permute-start.14 = (bf16[64,1024]{1,0:T(8,128)(2,1)S(1)}, bf16[64,1024]{1,0:T(8,128)(2,1)S(1)}, u32[]{:S(2)}, u32[]{:S(2)}) collective-permute-start(bf16[64,1024]{1,0:T(8,128)(2,1)S(1)} %get-tuple-element.66.refs_2_), channel_id=1, source_target_pairs={{0,1},{1,0},{2,3},{3,2},{4,5},{5,4},{6,7},{7,6},{8,9},{9,8},{10,11... | collective-permute-start | bytes 393224 | tf_op jit(solution)/shard_map/ppermute | solution.py:56
  31.5 10.2 %collective-permute-start.15 = (bf16[64,1024]{1,0:T(8,128)(2,1)S(1)}, bf16[64,1024]{1,0:T(8,128)(2,1)S(1)}, u32[]{:S(2)}, u32[]{:S(2)}) collective-permute-start(bf16[64,1024]{1,0:T(8,128)(2,1)S(1)} %get-tuple-element.66.refs_2_), channel_id=1, source_target_pairs={{0,2},{1,3},{2,0},{3,1},{4,6},{5,7},{6,4},{7,5},{8,10},{9,11},{10,... | collective-permute-start | bytes 393224 | tf_op jit(solution)/shard_map/ppermute | solution.py:56
  33.0 8.7 %collective-permute-start.16 = (bf16[64,1024]{1,0:T(8,128)(2,1)S(1)}, bf16[64,1024]{1,0:T(8,128)(2,1)S(1)}, u32[]{:S(2)}, u32[]{:S(2)}) collective-permute-start(bf16[64,1024]{1,0:T(8,128)(2,1)S(1)} %get-tuple-element.66.refs_2_), channel_id=1, source_target_pairs={{0,3},{1,2},{2,1},{3,0},{4,7},{5,6},{6,5},{7,4},{8,11},{9,10},{10,... | collective-permute-start | bytes 393224 | tf_op jit(solution)/shard_map/ppermute | solution.py:56
  43.1 8.0 %collective-permute-start.23 = (bf16[128,512]{1,0:T(8,128)(2,1)S(1)}, bf16[128,512]{1,0:T(8,128)(2,1)S(1)}, u32[]{:S(2)}, u32[]{:S(2)}) collective-permute-start(bf16[128,512]{1,0:T(8,128)(2,1)S(1)} %get-tuple-element.72), channel_id=1, source_target_pairs={{0,16},{4,20},{8,24},{12,28},{16,0},{20,4},{24,8},{28,12},{1,17},{... | collective-permute-start | bytes 393224 | tf_op jit(solution)/shard_map/ppermute | solution.py:476
  43.5 7.8 %collective-permute-start.20 = (bf16[64,512]{1,0:T(8,128)(2,1)S(1)}, bf16[64,512]{1,0:T(8,128)(2,1)S(1)}, u32[]{:S(2)}, u32[]{:S(2)}) collective-permute-start(bf16[64,512]{1,0:T(8,128)(2,1)S(1)} %get-tuple-element.69), channel_id=1, source_target_pairs={{0,4},{4,0},{8,12},{12,8},{16,20},{20,16},{24,28},{28,24},{1,5},{5... | collective-permute-start | bytes 196616 | tf_op jit(solution)/shard_map/ppermute | solution.py:56
  43.5 9.5 %collective-permute-start.21 = (bf16[64,512]{1,0:T(8,128)(2,1)S(1)}, bf16[64,512]{1,0:T(8,128)(2,1)S(1)}, u32[]{:S(2)}, u32[]{:S(2)}) collective-permute-start(bf16[64,512]{1,0:T(8,128)(2,1)S(1)} %get-tuple-element.70), channel_id=1, source_target_pairs={{0,8},{4,12},{8,0},{12,4},{16,24},{20,28},{24,16},{28,20},{1,9},{5... | collective-permute-start | bytes 196616 | tf_op jit(solution)/shard_map/ppermute | solution.py:56
  45.6 7.4 %collective-permute-start.22 = (bf16[64,512]{1,0:T(8,128)(2,1)S(1)}, bf16[64,512]{1,0:T(8,128)(2,1)S(1)}, u32[]{:S(2)}, u32[]{:S(2)}) collective-permute-start(bf16[64,512]{1,0:T(8,128)(2,1)S(1)} %get-tuple-element.71), channel_id=1, source_target_pairs={{0,12},{4,8},{8,4},{12,0},{16,28},{20,24},{24,20},{28,16},{1,13},{... | collective-permute-start | bytes 196616 | tf_op jit(solution)/shard_map/ppermute | solution.py:56
  51.1 1.9 %collective-permute-start.24 = (bf16[64,512]{1,0:T(8,128)(2,1)S(1)}, bf16[64,512]{1,0:T(8,128)(2,1)S(1)}, u32[]{:S(2)}, u32[]{:S(2)}) collective-permute-start(bf16[64,512]{1,0:T(8,128)(2,1)S(1)} %get-tuple-element.74), channel_id=1, source_target_pairs={{0,4},{4,0},{8,12},{12,8},{16,20},{20,16},{24,28},{28,24},{1,5},{5... | collective-permute-start | bytes 196616 | tf_op jit(solution)/shard_map/ppermute | solution.py:56
  51.2 5.0 %collective-permute-start.25 = (bf16[64,512]{1,0:T(8,128)(2,1)S(1)}, bf16[64,512]{1,0:T(8,128)(2,1)S(1)}, u32[]{:S(2)}, u32[]{:S(2)}) collective-permute-start(bf16[64,512]{1,0:T(8,128)(2,1)S(1)} %get-tuple-element.75), channel_id=1, source_target_pairs={{0,8},{4,12},{8,0},{12,4},{16,24},{20,28},{24,16},{28,20},{1,9},{5... | collective-permute-start | bytes 196616 | tf_op jit(solution)/shard_map/ppermute | solution.py:56
  51.2 5.3 %collective-permute-start.26 = (bf16[64,512]{1,0:T(8,128)(2,1)S(1)}, bf16[64,512]{1,0:T(8,128)(2,1)S(1)}, u32[]{:S(2)}, u32[]{:S(2)}) collective-permute-start(bf16[64,512]{1,0:T(8,128)(2,1)S(1)} %get-tuple-element.76), channel_id=1, source_target_pairs={{0,12},{4,8},{8,4},{12,0},{16,28},{20,24},{24,20},{28,16},{1,13},{... | collective-permute-start | bytes 196616 | tf_op jit(solution)/shard_map/ppermute | solution.py:56
where the time goes:
time: 57.8 us; the launch traced here: 57.7 us
  starting transfers between devices  27.7 us (48%)
  waiting for transfers between devices  22.4 us (39%)
  Pallas kernels  7.41 us (13%)
    ppermute x24, starting transfers between devices, rounds(): out[k] = lax.ppermute(x[k], axis, [(i, to(i, k, n)) for i in range(n)])  23.4 us
    ppermute x24, waiting for transfers between devices, rounds(): out[k] = lax.ppermute(x[k], axis, [(i, to(i, k, n)) for i in range(n)])  17.1 us
    ppermute x1, waiting for transfers between devices, on_device(): lax.ppermute(back, 'row', [(i, across(i, n)) for i in range(n)])  5.33 us
    ppermute x2, starting transfers between devices, gather(): lax.ppermute(out, 'row', [(i, across(i, n)) for i in range(n)])  3.86 us
    pallas_call x1, Pallas kernels, on_device(): pl.pallas_call(functools.partial(first_merge_kernel, n, slots), out_shape...  1.59 us
    pallas_call x1, Pallas kernels, on_device(): pl.pallas_call(functools.partial(attend_kernel, m, n_col), out_shape=[sha...  1.41 us
    pallas_call x2, Pallas kernels, project(): pl.pallas_call(functools.partial(project_kernel, m, rows, not tags), out_...  1.34 us
  transfers between devices with their start and end apart: 27, of which 11 were waited for; matrix products, arithmetic and copies ran while one was open for 0% of the time, Pallas kernels for 5%

commit v1 on v0

--- a/solution.py
+++ b/solution.py
@@ -66,7 +66,6 @@
 FIRST = (0, BLK // 2)
 SECOND = (BLK // 2, BLK - BLK // 2)
 PARTS = (FIRST, SECOND)
-HOME = ((0, BLK),)
 MESSAGES = (
     ((True, *FIRST),),
     ((True, *SECOND),),
@@ -209,12 +208,12 @@
             out_ref[s * (size // OWN) + h : s * (size // OWN) + h + rows, :] = pick[s]
 
 
-def project_kernel(m, rows, tagged, wq_ref, wk_ref, wv_ref, cross_ref, *refs):
+def project_kernel(m, rows, tagged, wk_ref, wv_ref, cross_ref, *refs):
     blocks, refs = refs[:m], refs[m:]
     if tagged:
-        q_ref, kv_ref, tag_ref, x_ref = refs
+        x_ref, kv_ref, tag_ref = refs
     else:
-        tag_ref, q_ref, kv_ref, x_ref = refs
+        tag_ref, x_ref, kv_ref = refs
     pieces = x_ref.shape[1] // LANES
     size = pieces * rows
     if tagged:
@@ -237,16 +236,35 @@
 
     kv_ref[:, :width] = mul(wk_ref)
     kv_ref[:, width:] = mul(wv_ref)
-    q_ref[...] = mul(wq_ref)
-
-
-def attend_kernel(m, n_col, tag_ref, bias_ref, *refs):
+
+
+def query_kernel(wq_ref, *refs):
+    xs, (q_ref,) = refs[:-1], refs[-1:]
+    x = jnp.concatenate(
+        [
+            xs[c][s * rows : (s + 1) * rows, :]
+            for s in range(OWN)
+            for c, (_, rows) in enumerate(PARTS)
+        ],
+        axis=0,
+    )
+    q = jnp.dot(x, wq_ref[...], preferred_element_type=jnp.float32).astype(jnp.bfloat16)
+    q = q * jnp.bfloat16(1.0 / math.sqrt(HD))
+    low = lax.broadcasted_iota(jnp.int32, (BLK, LANES), 1) < HD
+    zero = jnp.zeros((BLK, LANES), jnp.bfloat16)
+    for s in range(OWN):
+        for h in range(0, q.shape[1], LANES):
+            piece = q[s * BLK : (s + 1) * BLK, h : h + LANES]
+            at = 2 * s * BLK
+            q_ref[at : at + BLK, h : h + LANES] = jnp.where(low, piece, zero)
+            q_ref[at + BLK : at + 2 * BLK, h : h + LANES] = jnp.where(low, zero, piece)
+
+
+def attend_kernel(m, n_col, tag_ref, bias_ref, q_ref, *refs):
     refs = list(refs)
-    qs, refs = refs[: len(PARTS)], refs[len(PARTS) :]
     kvs, refs = refs[: len(PARTS) * n_col], refs[len(PARTS) * n_col :]
-    outs, backs, (head_ref,) = refs[:m], refs[m : m + len(HOME)], refs[m + len(HOME) :]
-    width = qs[0].shape[1]
-    scale = 1.0 / math.sqrt(HD)
+    outs, (back_ref, head_ref) = refs[:m], refs[m:]
+    width = q_ref.shape[1]
     low = lax.broadcasted_iota(jnp.int32, (BLK, LANES), 1) < HD
     zero = jnp.zeros((BLK, LANES), jnp.bfloat16)
     keys = bias_ref.shape[1]
@@ -254,25 +272,15 @@
         [jnp.broadcast_to(bias_ref[s : s + 1, :], (2 * BLK, keys)) for s in range(OWN)], axis=0
     )
     for h in range(0, width, LANES):
-        rows = []
-        for s in range(OWN):
-            q = jnp.concatenate(
-                [
-                    qs[c][s * size : (s + 1) * size, h : h + LANES]
-                    for c, (_, size) in enumerate(PARTS)
-                ],
-                axis=0,
-            )
-            rows += [jnp.where(low, q, zero), jnp.where(low, zero, q)]
         key = jnp.concatenate([kv[:, h : h + LANES] for kv in kvs], axis=0)
         value = jnp.concatenate([kv[:, width + h : width + h + LANES] for kv in kvs], axis=0)
         score = lax.dot_general(
-            jnp.concatenate(rows, axis=0),
+            q_ref[:, h : h + LANES],
             key,
             (((1,), (1,)), ((), ())),
             preferred_element_type=jnp.float32,
         )
-        score = score * scale + bias
+        score = score + bias
         p = jnp.exp(score - jnp.max(score, axis=1, keepdims=True))
         total = jnp.sum(p, axis=1, keepdims=True)
         o = jnp.dot(p.astype(jnp.bfloat16), value, preferred_element_type=jnp.float32)
@@ -282,9 +290,8 @@
             head_ref[s, :, h : h + LANES] = jnp.where(
                 low, o[at : at + BLK], o[at + BLK : at + 2 * BLK]
             )
-    for back, (start, rows) in zip(backs, HOME):
-        for s in range(OWN):
-            back[s * rows : (s + 1) * rows, :] = head_ref[s, start : start + rows, :]
+    for s in range(OWN):
+        back_ref[s * BLK : (s + 1) * BLK, :] = head_ref[s]
     masks = masks_of([tag_ref[k] for k in range(m)], BLK)
     for k in range(m):
         for h in range(0, width, LANES):
@@ -338,21 +345,27 @@
         out_ref[:, k0 : k0 + LANES] = jnp.transpose(hot).astype(jnp.bfloat16)
 
 
-def return_kernel(n, spread_ref, *refs):
-    m = n // 2
+def part_kernel(m, spread_ref, *refs):
+    blocks, (out_ref, all_ref) = refs[:m], refs[m:]
+    for k in range(m):
+        all_ref[k * BLK : (k + 1) * BLK, :] = blocks[k][...]
+    out_ref[...] = jnp.dot(
+        spread_ref[:, : m * BLK], all_ref[...], preferred_element_type=jnp.float32
+    ).astype(out_ref.dtype)
+
+
+def return_kernel(m, spread_ref, part_ref, *refs):
     blocks, (out_hbm, all_ref, out_ref, sems) = refs[:-4], refs[-4:]
     for k in range(m):
         all_ref[k * BLK : (k + 1) * BLK, :] = blocks[k][...]
-        for c, (start, rows) in enumerate(HOME):
-            at = (m + k) * BLK + start
-            all_ref[at : at + rows, :] = blocks[(1 + c) * m + k][...]
     step = out_ref.shape[0] // RETURN_STEPS
     copies = []
     for i in range(RETURN_STEPS):
         rows = slice(i * step, (i + 1) * step)
-        out_ref[rows, :] = jnp.dot(
-            spread_ref[rows, :], all_ref[...], preferred_element_type=jnp.float32
-        ).astype(out_ref.dtype)
+        far = jnp.dot(
+            spread_ref[rows, m * BLK :], all_ref[...], preferred_element_type=jnp.float32
+        )
+        out_ref[rows, :] = part_ref[rows, :] + far.astype(out_ref.dtype)
         copies.append(
             pltpu.make_async_copy(out_ref.at[rows, :], out_hbm.at[rows, :], sems.at[i])
         )
@@ -432,15 +445,14 @@
         rows = PARTS[c][1]
         out = pl.pallas_call(
             functools.partial(project_kernel, m, rows, not tags),
-            out_shape=[shape(OWN * rows, heads), shape(OWN * rows, 2 * heads)]
+            out_shape=[shape(OWN * rows, width), shape(OWN * rows, 2 * heads)]
             + [shape(m, TAG, LANES)] * (not tags),
-            in_specs=[VMEM] * (4 + m + len(tags)),
+            in_specs=[VMEM] * (3 + m + len(tags)),
             out_specs=[VMEM] * (2 + (not tags)),
-            scratch_shapes=[pltpu.VMEM((OWN * rows, width), bf16)],
             compiler_params=PARAMS,
             cost_estimate=cost(1),
             name="project",
-        )(w_query, w_key, w_value, cross, *blocks, *tags)
+        )(w_key, w_value, cross, *blocks, *tags)
         return out, rounds([out[1]] * n_col, "col", n_col, partner)
 
     far1 = rounds(far1, "row", n, inner)
@@ -448,9 +460,18 @@
     own0 = rounds(own0, "row", n, inner)
     own1 = rounds(own1, "row", n, inner)
     _, cross1 = gather(1, far1, known)
-    (q0, _, tags), kv0 = project(0, cross0, own0)
-    (q1, _), kv1 = project(1, cross1, own1, tags)
-    qs, kvs = [q0, q1], kv0 + kv1
+    (x0, _, tags), kv0 = project(0, cross0, own0)
+    (x1, _), kv1 = project(1, cross1, own1, tags)
+    kvs = kv0 + kv1
+    queries = pl.pallas_call(
+        query_kernel,
+        out_shape=shape(OWN * 2 * BLK, heads),
+        in_specs=[VMEM] * 3,
+        out_specs=VMEM,
+        compiler_params=PARAMS,
+        cost_estimate=cost(1),
+        name="query",
+    )(w_query, x0, x1)
     spread, bias = pl.pallas_call(
         functools.partial(spread_kernel, n, n_col, slots),
         out_shape=[
@@ -465,42 +486,51 @@
     )(map_in, block_owner, neighbours)
     outs = pl.pallas_call(
         functools.partial(attend_kernel, m, n_col),
-        out_shape=[shape(BLK, heads)] * m + [shape(OWN * rows, heads) for _, rows in HOME],
-        in_specs=[VMEM] * (2 + len(qs) + len(kvs)),
-        out_specs=[VMEM] * (m + len(HOME)),
+        out_shape=[shape(BLK, heads)] * m + [shape(OWN * BLK, heads)],
+        in_specs=[VMEM] * (3 + len(kvs)),
+        out_specs=[VMEM] * (m + 1),
         scratch_shapes=[pltpu.VMEM((OWN, BLK, heads), bf16)],
         compiler_params=PARAMS,
         cost_estimate=cost(3),
         name="attend",
-    )(tags, bias, *qs, *kvs)
-    backs = [lax.ppermute(back, "row", [(i, across(i, n)) for i in range(n)]) for back in outs[m:]]
+    )(tags, bias, queries, *kvs)
+    back = lax.ppermute(outs[m], "row", [(i, across(i, n)) for i in range(n)])
     to_sender = functools.partial(inner, back=True)
-    returned = rounds(outs[:m], "row", n, to_sender)
-    for c, (_, rows) in enumerate(HOME):
-        relayed = pl.pallas_call(
-            functools.partial(relay_kernel, m),
-            out_shape=[shape(rows, heads)] * m,
-            in_specs=[VMEM] * 2,
-            out_specs=[VMEM] * m,
-            compiler_params=PARAMS,
-            cost_estimate=cost(0.5),
-            name="relay",
-        )(known, backs[c])
-        returned += rounds(relayed, "row", n, to_sender)
+    homes = rounds(outs[:m], "row", n, to_sender)
+    relayed = pl.pallas_call(
+        functools.partial(relay_kernel, m),
+        out_shape=[shape(BLK, heads)] * m,
+        in_specs=[VMEM] * 2,
+        out_specs=[VMEM] * m,
+        compiler_params=PARAMS,
+        cost_estimate=cost(0.5),
+        name="relay",
+    )(known, back)
+    relayed = rounds(relayed, "row", n, to_sender)
+    part = pl.pallas_call(
+        functools.partial(part_kernel, m),
+        out_shape=shape(toks, heads),
+        in_specs=[VMEM] * (1 + m),
+        out_specs=VMEM,
+        scratch_shapes=[pltpu.VMEM((m * BLK, heads), bf16)],
+        compiler_params=PARAMS,
+        cost_estimate=cost(1),
+        name="part",
+    )(spread, *homes)
     return pl.pallas_call(
-        functools.partial(return_kernel, n),
+        functools.partial(return_kernel, m),
         out_shape=shape(toks, heads),
-        in_specs=[VMEM] * (1 + len(returned)),
+        in_specs=[VMEM] * (2 + m),
         out_specs=HBM,
         scratch_shapes=[
-            pltpu.VMEM((n * BLK, heads), bf16),
+            pltpu.VMEM((m * BLK, heads), bf16),
             pltpu.VMEM((toks, heads), bf16),
             pltpu.SemaphoreType.DMA((RETURN_STEPS,)),
         ],
         compiler_params=PARAMS,
         cost_estimate=cost(2),
         name="give_back",
-    )(spread, *returned)
+    )(spread, part, *relayed)
 
 
 def solution(mesh):

time: 57.8 us -> 57.5 us (level)
    pallas_call x2 -> x4, Pallas kernels: 1.2 us -> 1.71 us  [the longest x1 1.03 us: on_device(): pl.pallas_call(functools.partial(return_kernel, m), out_shape=shape(toks,...]
where the time goes in v1:
time: 57.5 us; the launch traced here: 57.4 us
  starting transfers between devices  27.7 us (48%)
  waiting for transfers between devices  22 us (38%)
  Pallas kernels  7.57 us (13%)
    ppermute x24, starting transfers between devices, rounds(): out[k] = lax.ppermute(x[k], axis, [(i, to(i, k, n)) for i in range(n)])  23.4 us
    ppermute x24, waiting for transfers between devices, rounds(): out[k] = lax.ppermute(x[k], axis, [(i, to(i, k, n)) for i in range(n)])  16.6 us
    ppermute x1, waiting for transfers between devices, on_device(): back = lax.ppermute(outs[m], 'row', [(i, across(i, n)) for i in range(n)])  5.33 us
    ppermute x2, starting transfers between devices, gather(): lax.ppermute(out, 'row', [(i, across(i, n)) for i in range(n)])  3.86 us
    pallas_call x1, Pallas kernels, on_device(): pl.pallas_call(functools.partial(first_merge_kernel, n, slots), out_shape...  1.59 us
    pallas_call x1, Pallas kernels, on_device(): pl.pallas_call(functools.partial(attend_kernel, m, n_col), out_shape=[sha...  1.43 us
  transfers between devices with their start and end apart: 27, of which 11 were waited for; matrix products, arithmetic and copies ran while one was open for 0% of the time, Pallas kernels for 5%

profile of v1, /device:TPU:0, one launch (start us, length us, event | category | flops | bytes accessed | tf_op | source)
XLA Modules:
  0.0 57.4 jit_solution(8102895854263482008)
XLA Ops:
  0.0 1.6 %merge.1 = (bf16[264,128]{1,0:T(8,128)(2,1)S(1)}, bf16[264,128]{1,0:T(8,128)(2,1)S(1)}, bf16[264,128]{1,0:T(8,128)(2,1)S(1)}, bf16[264,128]{1,0:T(8,128)(2,1)S(1...) custom-call(bf16[512,1024]{1,0:T(8,128)(2,1)} %tok_hbm.1, ...), custom_call_target="tpu_custom_call" | custom-call | flops 1600000000 | bytes 4000000 | tf_op jit(solution)/shard_map/merge/pallas_call | solution.py:400
  1.6 0.6 collective-permute-start
  2.2 2.6 %collective-permute-start.1 = (bf16[264,128]{1,0:T(8,128)(2,1)S(1)}, bf16[264,128]{1,0:T(8,128)(2,1)S(1)}, u32[]{:S(2)}, u32[]{:S(2)}) collective-permute-start(bf16[264,128]{1,0:T(8,128)(2,1)S(1)} %get-tuple-element.45), channel_id=1, source_target_pairs={{0,8},{4,12},{8,0},{12,4},{16,24},{20,28},{24,16},{28,20},{1,9},{5... | collective-permute-start | bytes 202760 | tf_op jit(solution)/shard_map/ppermute | solution.py:56
  4.8 0.7 %merge_rest.1 = (bf16[256,128]{1,0:T(8,128)(2,1)S(1)}, bf16[256,128]{1,0:T(8,128)(2,1)S(1)}, bf16[256,128]{1,0:T(8,128)(2,1)S(1)}, bf16[256,128]{1,0:T(8,128)(2,...) custom-call(bf16[512,1024]{1,0:T(8,128)(2,1)S(1)} %get-tuple-element, ...), custom_call_target="tpu_custom_call" | custom-call | flops 1600000000 | bytes 4000000 | tf_op jit(solution)/shard_map/merge_rest/pallas_call | solution.py:420
  5.8 1.9 %collective-permute-start.8 = (bf16[256,128]{1,0:T(8,128)(2,1)S(1)}, bf16[256,128]{1,0:T(8,128)(2,1)S(1)}, u32[]{:S(2)}, u32[]{:S(2)}) collective-permute-start(bf16[256,128]{1,0:T(8,128)(2,1)S(1)} %get-tuple-element.59), channel_id=1, source_target_pairs={{0,8},{4,12},{8,0},{12,4},{16,24},{20,28},{24,16},{28,20},{1,9},{5... | collective-permute-start | bytes 196616 | tf_op jit(solution)/shard_map/ppermute | solution.py:56
  7.7 1.2 %collective-permute-done.2.refs_3_ = bf16[264,128]{1,0:T(8,128)(2,1)S(1)} collective-permute-done((bf16[264,128]{1,0:T(8,128)(2,1)S(1)}, bf16[264,128]{1,0:T(8,128)(2,1)S(1)}, u32[]{:S(2)}, u32[]{:S(2)}) %collective-permute-start.2) | collective-permute-done | bytes 67616 | tf_op jit(solution)/shard_map/ppermute | solution.py:56
  9.0 2.7 %collective-permute-start.3 = (bf16[520,128]{1,0:T(8,128)(2,1)S(1)}, bf16[520,128]{1,0:T(8,128)(2,1)S(1)}, u32[]{:S(2)}, u32[]{:S(2)}) collective-permute-start(bf16[520,128]{1,0:T(8,128)(2,1)S(1)} %gather.2.refs_4_.known_ref), channel_id=1, source_target_pairs={{0,16},{4,20},{8,24},{12,28},{16,0},{20,4},{24,8},{28,12},{1,17},{... | collective-permute-start | bytes 399368 | tf_op jit(solution)/shard_map/ppermute | solution.py:442
  11.8 1.4 %collective-permute-start.5 = (bf16[264,128]{1,0:T(8,128)(2,1)S(1)}, bf16[264,128]{1,0:T(8,128)(2,1)S(1)}, u32[]{:S(2)}, u32[]{:S(2)}) collective-permute-start(bf16[264,128]{1,0:T(8,128)(2,1)S(1)} %get-tuple-element.52), channel_id=1, source_target_pairs={{0,8},{4,12},{8,0},{12,4},{16,24},{20,28},{24,16},{28,20},{1,9},{5... | collective-permute-start | bytes 202760 | tf_op jit(solution)/shard_map/ppermute | solution.py:56
  13.5 1.2 %collective-permute-start.10 = (bf16[512,128]{1,0:T(8,128)(2,1)S(1)}, bf16[512,128]{1,0:T(8,128)(2,1)S(1)}, u32[]{:S(2)}, u32[]{:S(2)}) collective-permute-start(bf16[512,128]{1,0:T(8,128)(2,1)S(1)} %gather.3), channel_id=1, source_target_pairs={{0,16},{4,20},{8,24},{12,28},{16,0},{20,4},{24,8},{28,12},{1,17},{... | collective-permute-start | bytes 393224 | tf_op jit(solution)/shard_map/ppermute | solution.py:442
  14.8 0.5 collective-permute-start.11
  15.2 1.8 %collective-permute-done.5.refs_2_ = bf16[264,128]{1,0:T(8,128)(2,1)S(1)} collective-permute-done((bf16[264,128]{1,0:T(8,128)(2,1)S(1)}, bf16[264,128]{1,0:T(8,128)(2,1)S(1)}, u32[]{:S(2)}, u32[]{:S(2)}) %collective-permute-start.5) | collective-permute-done | bytes 67616 | tf_op jit(solution)/shard_map/ppermute | solution.py:56
  17.1 2.5 %collective-permute-start.12 = (bf16[256,128]{1,0:T(8,128)(2,1)S(1)}, bf16[256,128]{1,0:T(8,128)(2,1)S(1)}, u32[]{:S(2)}, u32[]{:S(2)}) collective-permute-start(bf16[256,128]{1,0:T(8,128)(2,1)S(1)} %get-tuple-element.63), channel_id=1, source_target_pairs={{0,8},{4,12},{8,0},{12,4},{16,24},{20,28},{24,16},{28,20},{1,9},{5... | collective-permute-start | bytes 196616 | tf_op jit(solution)/shard_map/ppermute | solution.py:56
  19.5 1.0 %collective-permute-done.6.refs_3_ = bf16[264,128]{1,0:T(8,128)(2,1)S(1)} collective-permute-done((bf16[264,128]{1,0:T(8,128)(2,1)S(1)}, bf16[264,128]{1,0:T(8,128)(2,1)S(1)}, u32[]{:S(2)}, u32[]{:S(2)}) %collective-permute-start.6) | collective-permute-done | bytes 67616 | tf_op jit(solution)/shard_map/ppermute | solution.py:56
  20.7 0.5 project.2
  21.2 1.5 %collective-permute-done.12.refs_2_ = bf16[256,128]{1,0:T(8,128)(2,1)S(1)} collective-permute-done((bf16[256,128]{1,0:T(8,128)(2,1)S(1)}, bf16[256,128]{1,0:T(8,128)(2,1)S(1)}, u32[]{:S(2)}, u32[]{:S(2)}) %collective-permute-start.12) | collective-permute-done | bytes 65568 | tf_op jit(solution)/shard_map/ppermute | solution.py:56
  22.8 3.0 %collective-permute-done.13.refs_3_ = bf16[256,128]{1,0:T(8,128)(2,1)S(1)} collective-permute-done((bf16[256,128]{1,0:T(8,128)(2,1)S(1)}, bf16[256,128]{1,0:T(8,128)(2,1)S(1)}, u32[]{:S(2)}, u32[]{:S(2)}) %collective-permute-start.13) | collective-permute-done | bytes 65568 | tf_op jit(solution)/shard_map/ppermute | solution.py:56
  25.8 0.5 project.3
  26.2 1.6 %collective-permute-start.17 = (bf16[64,1024]{1,0:T(8,128)(2,1)S(1)}, bf16[64,1024]{1,0:T(8,128)(2,1)S(1)}, u32[]{:S(2)}, u32[]{:S(2)}) collective-permute-start(bf16[64,1024]{1,0:T(8,128)(2,1)S(1)} %get-tuple-element.67.refs_4_), channel_id=1, source_target_pairs={{0,1},{1,0},{2,3},{3,2},{4,5},{5,4},{6,7},{7,6},{8,9},{9,8},{10,11... | collective-permute-start | bytes 393224 | tf_op jit(solution)/shard_map/ppermute | solution.py:56
  27.8 1.5 %collective-permute-start.18 = (bf16[64,1024]{1,0:T(8,128)(2,1)S(1)}, bf16[64,1024]{1,0:T(8,128)(2,1)S(1)}, u32[]{:S(2)}, u32[]{:S(2)}) collective-permute-start(bf16[64,1024]{1,0:T(8,128)(2,1)S(1)} %get-tuple-element.67.refs_4_), channel_id=1, source_target_pairs={{0,2},{1,3},{2,0},{3,1},{4,6},{5,7},{6,4},{7,5},{8,10},{9,11},{10,... | collective-permute-start | bytes 393224 | tf_op jit(solution)/shard_map/ppermute | solution.py:56
  29.3 0.5 collective-permute-start.19
  29.8 1.5 %collective-permute-start.14 = (bf16[64,1024]{1,0:T(8,128)(2,1)S(1)}, bf16[64,1024]{1,0:T(8,128)(2,1)S(1)}, u32[]{:S(2)}, u32[]{:S(2)}) collective-permute-start(bf16[64,1024]{1,0:T(8,128)(2,1)S(1)} %get-tuple-element.66.refs_0_), channel_id=1, source_target_pairs={{0,1},{1,0},{2,3},{3,2},{4,5},{5,4},{6,7},{7,6},{8,9},{9,8},{10,11... | collective-permute-start | bytes 393224 | tf_op jit(solution)/shard_map/ppermute | solution.py:56
  31.3 1.5 %collective-permute-start.15 = (bf16[64,1024]{1,0:T(8,128)(2,1)S(1)}, bf16[64,1024]{1,0:T(8,128)(2,1)S(1)}, u32[]{:S(2)}, u32[]{:S(2)}) collective-permute-start(bf16[64,1024]{1,0:T(8,128)(2,1)S(1)} %get-tuple-element.66.refs_0_), channel_id=1, source_target_pairs={{0,2},{1,3},{2,0},{3,1},{4,6},{5,7},{6,4},{7,5},{8,10},{9,11},{10,... | collective-permute-start | bytes 393224 | tf_op jit(solution)/shard_map/ppermute | solution.py:56
  32.8 2.3 %collective-permute-start.16 = (bf16[64,1024]{1,0:T(8,128)(2,1)S(1)}, bf16[64,1024]{1,0:T(8,128)(2,1)S(1)}, u32[]{:S(2)}, u32[]{:S(2)}) collective-permute-start(bf16[64,1024]{1,0:T(8,128)(2,1)S(1)} %get-tuple-element.66.refs_0_), channel_id=1, source_target_pairs={{0,3},{1,2},{2,1},{3,0},{4,7},{5,6},{6,5},{7,4},{8,11},{9,10},{10,... | collective-permute-start | bytes 393224 | tf_op jit(solution)/shard_map/ppermute | solution.py:56
  35.1 1.1 %spread.1 = (bf16[512,512]{1,0:T(8,128)(2,1)S(1)}, f32[8,512]{1,0:T(8,128)S(1)}) custom-call(s32[1,512]{1,0:T(1,128)S(1)} %get-tuple-element.41.map_ref, s32[1,8]{1,0:T(1,128)} %owner_ref.1, s32[2,4]{1,0:T(2,128)} %near_ref.1), custom_call_target="tpu_custom_call" | custom-call | flops 1600000000 | bytes 4000000 | tf_op jit(solution)/shard_map/spread/pallas_call | solution.py:475
  36.6 1.8 %collective-permute-done.14.refs_1_ = bf16[64,1024]{1,0:T(8,128)(2,1)S(1)} collective-permute-done((bf16[64,1024]{1,0:T(8,128)(2,1)S(1)}, bf16[64,1024]{1,0:T(8,128)(2,1)S(1)}, u32[]{:S(2)}, u32[]{:S(2)}) %collective-permute-start.14) | collective-permute-done | bytes 131104 | tf_op jit(solution)/shard_map/ppermute | solution.py:56
  38.5 3.0 %collective-permute-done.15.refs_2_ = bf16[64,1024]{1,0:T(8,128)(2,1)S(1)} collective-permute-done((bf16[64,1024]{1,0:T(8,128)(2,1)S(1)}, bf16[64,1024]{1,0:T(8,128)(2,1)S(1)}, u32[]{:S(2)}, u32[]{:S(2)}) %collective-permute-start.15) | collective-permute-done | bytes 131104 | tf_op jit(solution)/shard_map/ppermute | solution.py:56
  41.5 1.4 %attend.1 = (bf16[64,512]{1,0:T(8,128)(2,1)S(1)}, bf16[64,512]{1,0:T(8,128)(2,1)S(1)}, bf16[64,512]{1,0:T(8,128)(2,1)S(1)}, bf16[64,512]{1,0:T(8,128)(2,1)S(1)}, bf16[128,512]{1,0:T(8,128)(2,1)S(1)}) custom-call(bf16[4,8,128]{2,1,0:T(8,128)(2,1)S(1)} %get-tuple-element.54.refs_4_.tag_ref, f32[8,512]{1,0:T(8,128)S(1)} %get-tuple-element.55.bias_ref, ...), custom_call_target="tpu_custom_call" | custom-call | flops 2400000000 | bytes 6000000 | tf_op jit(solution)/shard_map/attend/pallas_call | solution.py:487
  43.3 2.1 %collective-permute-start.21 = (bf16[64,512]{1,0:T(8,128)(2,1)S(1)}, bf16[64,512]{1,0:T(8,128)(2,1)S(1)}, u32[]{:S(2)}, u32[]{:S(2)}) collective-permute-start(bf16[64,512]{1,0:T(8,128)(2,1)S(1)} %get-tuple-element.70), channel_id=1, source_target_pairs={{0,8},{4,12},{8,0},{12,4},{16,24},{20,28},{24,16},{28,20},{1,9},{5... | collective-permute-start | bytes 196616 | tf_op jit(solution)/shard_map/ppermute | solution.py:56
  45.5 5.3 %collective-permute-done.23.back_ref = bf16[128,512]{1,0:T(8,128)(2,1)S(1)} collective-permute-done((bf16[128,512]{1,0:T(8,128)(2,1)S(1)}, bf16[128,512]{1,0:T(8,128)(2,1)S(1)}, u32[]{:S(2)}, u32[]{:S(2)}) %collective-permute-start.23) | collective-permute-done | bytes 131104 | tf_op jit(solution)/shard_map/ppermute | solution.py:497
  51.1 1.8 %collective-permute-start.26 = (bf16[64,512]{1,0:T(8,128)(2,1)S(1)}, bf16[64,512]{1,0:T(8,128)(2,1)S(1)}, u32[]{:S(2)}, u32[]{:S(2)}) collective-permute-start(bf16[64,512]{1,0:T(8,128)(2,1)S(1)} %get-tuple-element.76), channel_id=1, source_target_pairs={{0,12},{4,8},{8,4},{12,0},{16,28},{20,24},{24,20},{28,16},{1,13},{... | collective-permute-start | bytes 196616 | tf_op jit(solution)/shard_map/ppermute | solution.py:56
  53.2 2.9 %collective-permute-done.25.refs_2_ = bf16[64,512]{1,0:T(8,128)(2,1)S(1)} collective-permute-done((bf16[64,512]{1,0:T(8,128)(2,1)S(1)}, bf16[64,512]{1,0:T(8,128)(2,1)S(1)}, u32[]{:S(2)}, u32[]{:S(2)}) %collective-permute-start.25) | collective-permute-done | bytes 65568 | tf_op jit(solution)/shard_map/ppermute | solution.py:56
  56.4 1.0 %give_back.1 = bf16[512,512]{1,0:T(8,128)(2,1)} custom-call(bf16[512,512]{1,0:T(8,128)(2,1)S(1)} %get-tuple-element.42.spread_ref, bf16[512,512]{1,0:T(8,128)(2,1)S(1)} %part.1.part_ref, bf16[64,512]{1,0:T(8,128)(2,1)S(1)} %get-tuple-element.73.refs_0_, bf16[64,512]{1,0:T(8,128)(2,1)S(1)} %collective-permute-done.24.refs_1_, ...), custom_call_target="tpu_custom_call" | custom-call | flops 1600000000 | bytes 4000000 | tf_op jit(solution)/shard_map/give_back/pallas_call | solution.py:520
  (40 shorter events, 2.8 us)
Async XLA Ops:
  1.6 6.1 %collective-permute-start = (bf16[264,128]{1,0:T(8,128)(2,1)S(1)}, bf16[264,128]{1,0:T(8,128)(2,1)S(1)}, u32[]{:S(2)}, u32[]{:S(2)}) collective-permute-start(bf16[264,128]{1,0:T(8,128)(2,1)S(1)} %get-tuple-element.44), channel_id=1, source_target_pairs={{0,4},{4,0},{8,12},{12,8},{16,20},{20,16},{24,28},{28,24},{1,5},{5... | collective-permute-start | bytes 202760 | tf_op jit(solution)/shard_map/ppermute | solution.py:56
  2.2 5.6 %collective-permute-start.1 = (bf16[264,128]{1,0:T(8,128)(2,1)S(1)}, bf16[264,128]{1,0:T(8,128)(2,1)S(1)}, u32[]{:S(2)}, u32[]{:S(2)}) collective-permute-start(bf16[264,128]{1,0:T(8,128)(2,1)S(1)} %get-tuple-element.45), channel_id=1, source_target_pairs={{0,8},{4,12},{8,0},{12,4},{16,24},{20,28},{24,16},{28,20},{1,9},{5... | collective-permute-start | bytes 202760 | tf_op jit(solution)/shard_map/ppermute | solution.py:56
  4.8 4.1 %collective-permute-start.2 = (bf16[264,128]{1,0:T(8,128)(2,1)S(1)}, bf16[264,128]{1,0:T(8,128)(2,1)S(1)}, u32[]{:S(2)}, u32[]{:S(2)}) collective-permute-start(bf16[264,128]{1,0:T(8,128)(2,1)S(1)} %get-tuple-element.46), channel_id=1, source_target_pairs={{0,12},{4,8},{8,4},{12,0},{16,28},{20,24},{24,20},{28,16},{1,13},{... | collective-permute-start | bytes 202760 | tf_op jit(solution)/shard_map/ppermute | solution.py:56
  5.5 6.3 %collective-permute-start.7 = (bf16[256,128]{1,0:T(8,128)(2,1)S(1)}, bf16[256,128]{1,0:T(8,128)(2,1)S(1)}, u32[]{:S(2)}, u32[]{:S(2)}) collective-permute-start(bf16[256,128]{1,0:T(8,128)(2,1)S(1)} %get-tuple-element.58), channel_id=1, source_target_pairs={{0,4},{4,0},{8,12},{12,8},{16,20},{20,16},{24,28},{28,24},{1,5},{5... | collective-permute-start | bytes 196616 | tf_op jit(solution)/shard_map/ppermute | solution.py:56
  5.8 7.5 %collective-permute-start.8 = (bf16[256,128]{1,0:T(8,128)(2,1)S(1)}, bf16[256,128]{1,0:T(8,128)(2,1)S(1)}, u32[]{:S(2)}, u32[]{:S(2)}) collective-permute-start(bf16[256,128]{1,0:T(8,128)(2,1)S(1)} %get-tuple-element.59), channel_id=1, source_target_pairs={{0,8},{4,12},{8,0},{12,4},{16,24},{20,28},{24,16},{28,20},{1,9},{5... | collective-permute-start | bytes 196616 | tf_op jit(solution)/shard_map/ppermute | solution.py:56
  7.7 5.8 %collective-permute-start.9 = (bf16[256,128]{1,0:T(8,128)(2,1)S(1)}, bf16[256,128]{1,0:T(8,128)(2,1)S(1)}, u32[]{:S(2)}, u32[]{:S(2)}) collective-permute-start(bf16[256,128]{1,0:T(8,128)(2,1)S(1)} %get-tuple-element.60), channel_id=1, source_target_pairs={{0,12},{4,8},{8,4},{12,0},{16,28},{20,24},{24,20},{28,16},{1,13},{... | collective-permute-start | bytes 196616 | tf_op jit(solution)/shard_map/ppermute | solution.py:56
  8.9 11.8 %copy-start.1 = (bf16[1024,512]{1,0:T(8,128)(2,1)S(1)}, bf16[1024,512]{1,0:T(8,128)(2,1)}, u32[]{:S(2)}) copy-start(bf16[1024,512]{1,0:T(8,128)(2,1)} %wv_ref.3) | copy-start | bytes 3145732
  9.0 11.8 %copy-start = (bf16[1024,512]{1,0:T(8,128)(2,1)S(1)}, bf16[1024,512]{1,0:T(8,128)(2,1)}, u32[]{:S(2)}) copy-start(bf16[1024,512]{1,0:T(8,128)(2,1)} %wk_ref.3) | copy-start | bytes 3145732
  9.0 11.7 %collective-permute-start.3 = (bf16[520,128]{1,0:T(8,128)(2,1)S(1)}, bf16[520,128]{1,0:T(8,128)(2,1)S(1)}, u32[]{:S(2)}, u32[]{:S(2)}) collective-permute-start(bf16[520,128]{1,0:T(8,128)(2,1)S(1)} %gather.2.refs_4_.known_ref), channel_id=1, source_target_pairs={{0,16},{4,20},{8,24},{12,28},{16,0},{20,4},{24,8},{28,12},{1,17},{... | collective-permute-start | bytes 399368 | tf_op jit(solution)/shard_map/ppermute | solution.py:442
  11.6 3.1 %collective-permute-start.4 = (bf16[264,128]{1,0:T(8,128)(2,1)S(1)}, bf16[264,128]{1,0:T(8,128)(2,1)S(1)}, u32[]{:S(2)}, u32[]{:S(2)}) collective-permute-start(bf16[264,128]{1,0:T(8,128)(2,1)S(1)} %get-tuple-element.51), channel_id=1, source_target_pairs={{0,4},{4,0},{8,12},{12,8},{16,20},{20,16},{24,28},{28,24},{1,5},{5... | collective-permute-start | bytes 202760 | tf_op jit(solution)/shard_map/ppermute | solution.py:56
  11.8 5.2 %collective-permute-start.5 = (bf16[264,128]{1,0:T(8,128)(2,1)S(1)}, bf16[264,128]{1,0:T(8,128)(2,1)S(1)}, u32[]{:S(2)}, u32[]{:S(2)}) collective-permute-start(bf16[264,128]{1,0:T(8,128)(2,1)S(1)} %get-tuple-element.52), channel_id=1, source_target_pairs={{0,8},{4,12},{8,0},{12,4},{16,24},{20,28},{24,16},{28,20},{1,9},{5... | collective-permute-start | bytes 202760 | tf_op jit(solution)/shard_map/ppermute | solution.py:56
  13.3 7.3 %collective-permute-start.6 = (bf16[264,128]{1,0:T(8,128)(2,1)S(1)}, bf16[264,128]{1,0:T(8,128)(2,1)S(1)}, u32[]{:S(2)}, u32[]{:S(2)}) collective-permute-start(bf16[264,128]{1,0:T(8,128)(2,1)S(1)} %get-tuple-element.53), channel_id=1, source_target_pairs={{0,12},{4,8},{8,4},{12,0},{16,28},{20,24},{24,20},{28,16},{1,13},{... | collective-permute-start | bytes 202760 | tf_op jit(solution)/shard_map/ppermute | solution.py:56
  13.5 12.2 %collective-permute-start.10 = (bf16[512,128]{1,0:T(8,128)(2,1)S(1)}, bf16[512,128]{1,0:T(8,128)(2,1)S(1)}, u32[]{:S(2)}, u32[]{:S(2)}) collective-permute-start(bf16[512,128]{1,0:T(8,128)(2,1)S(1)} %gather.3), channel_id=1, source_target_pairs={{0,16},{4,20},{8,24},{12,28},{16,0},{20,4},{24,8},{28,12},{1,17},{... | collective-permute-start | bytes 393224 | tf_op jit(solution)/shard_map/ppermute | solution.py:442
  14.8 6.5 %collective-permute-start.11 = (bf16[256,128]{1,0:T(8,128)(2,1)S(1)}, bf16[256,128]{1,0:T(8,128)(2,1)S(1)}, u32[]{:S(2)}, u32[]{:S(2)}) collective-permute-start(bf16[256,128]{1,0:T(8,128)(2,1)S(1)} %get-tuple-element.62), channel_id=1, source_target_pairs={{0,4},{4,0},{8,12},{12,8},{16,20},{20,16},{24,28},{28,24},{1,5},{5... | collective-permute-start | bytes 196616 | tf_op jit(solution)/shard_map/ppermute | solution.py:56
  17.1 5.7 %collective-permute-start.12 = (bf16[256,128]{1,0:T(8,128)(2,1)S(1)}, bf16[256,128]{1,0:T(8,128)(2,1)S(1)}, u32[]{:S(2)}, u32[]{:S(2)}) collective-permute-start(bf16[256,128]{1,0:T(8,128)(2,1)S(1)} %get-tuple-element.63), channel_id=1, source_target_pairs={{0,8},{4,12},{8,0},{12,4},{16,24},{20,28},{24,16},{28,20},{1,9},{5... | collective-permute-start | bytes 196616 | tf_op jit(solution)/shard_map/ppermute | solution.py:56
  20.5 5.2 %collective-permute-start.13 = (bf16[256,128]{1,0:T(8,128)(2,1)S(1)}, bf16[256,128]{1,0:T(8,128)(2,1)S(1)}, u32[]{:S(2)}, u32[]{:S(2)}) collective-permute-start(bf16[256,128]{1,0:T(8,128)(2,1)S(1)} %get-tuple-element.64), channel_id=1, source_target_pairs={{0,12},{4,8},{8,4},{12,0},{16,28},{20,24},{24,20},{28,16},{1,13},{... | collective-permute-start | bytes 196616 | tf_op jit(solution)/shard_map/ppermute | solution.py:56
  26.2 6.6 %collective-permute-start.17 = (bf16[64,1024]{1,0:T(8,128)(2,1)S(1)}, bf16[64,1024]{1,0:T(8,128)(2,1)S(1)}, u32[]{:S(2)}, u32[]{:S(2)}) collective-permute-start(bf16[64,1024]{1,0:T(8,128)(2,1)S(1)} %get-tuple-element.67.refs_4_), channel_id=1, source_target_pairs={{0,1},{1,0},{2,3},{3,2},{4,5},{5,4},{6,7},{7,6},{8,9},{9,8},{10,11... | collective-permute-start | bytes 393224 | tf_op jit(solution)/shard_map/ppermute | solution.py:56
  27.8 8.8 %collective-permute-start.18 = (bf16[64,1024]{1,0:T(8,128)(2,1)S(1)}, bf16[64,1024]{1,0:T(8,128)(2,1)S(1)}, u32[]{:S(2)}, u32[]{:S(2)}) collective-permute-start(bf16[64,1024]{1,0:T(8,128)(2,1)S(1)} %get-tuple-element.67.refs_4_), channel_id=1, source_target_pairs={{0,2},{1,3},{2,0},{3,1},{4,6},{5,7},{6,4},{7,5},{8,10},{9,11},{10,... | collective-permute-start | bytes 393224 | tf_op jit(solution)/shard_map/ppermute | solution.py:56
  29.3 7.3 %collective-permute-start.19 = (bf16[64,1024]{1,0:T(8,128)(2,1)S(1)}, bf16[64,1024]{1,0:T(8,128)(2,1)S(1)}, u32[]{:S(2)}, u32[]{:S(2)}) collective-permute-start(bf16[64,1024]{1,0:T(8,128)(2,1)S(1)} %get-tuple-element.67.refs_4_), channel_id=1, source_target_pairs={{0,3},{1,2},{2,1},{3,0},{4,7},{5,6},{6,5},{7,4},{8,11},{9,10},{10,... | collective-permute-start | bytes 393224 | tf_op jit(solution)/shard_map/ppermute | solution.py:56
  29.8 6.4 %copy-start.2 = (bf16[1024,512]{1,0:T(8,128)(2,1)S(1)}, bf16[1024,512]{1,0:T(8,128)(2,1)}, u32[]{:S(2)}) copy-start(bf16[1024,512]{1,0:T(8,128)(2,1)} %wq_ref.1) | copy-start | bytes 3145732
  29.8 8.7 %collective-permute-start.14 = (bf16[64,1024]{1,0:T(8,128)(2,1)S(1)}, bf16[64,1024]{1,0:T(8,128)(2,1)S(1)}, u32[]{:S(2)}, u32[]{:S(2)}) collective-permute-start(bf16[64,1024]{1,0:T(8,128)(2,1)S(1)} %get-tuple-element.66.refs_0_), channel_id=1, source_target_pairs={{0,1},{1,0},{2,3},{3,2},{4,5},{5,4},{6,7},{7,6},{8,9},{9,8},{10,11... | collective-permute-start | bytes 393224 | tf_op jit(solution)/shard_map/ppermute | solution.py:56
  31.3 10.2 %collective-permute-start.15 = (bf16[64,1024]{1,0:T(8,128)(2,1)S(1)}, bf16[64,1024]{1,0:T(8,128)(2,1)S(1)}, u32[]{:S(2)}, u32[]{:S(2)}) collective-permute-start(bf16[64,1024]{1,0:T(8,128)(2,1)S(1)} %get-tuple-element.66.refs_0_), channel_id=1, source_target_pairs={{0,2},{1,3},{2,0},{3,1},{4,6},{5,7},{6,4},{7,5},{8,10},{9,11},{10,... | collective-permute-start | bytes 393224 | tf_op jit(solution)/shard_map/ppermute | solution.py:56
  32.8 8.7 %collective-permute-start.16 = (bf16[64,1024]{1,0:T(8,128)(2,1)S(1)}, bf16[64,1024]{1,0:T(8,128)(2,1)S(1)}, u32[]{:S(2)}, u32[]{:S(2)}) collective-permute-start(bf16[64,1024]{1,0:T(8,128)(2,1)S(1)} %get-tuple-element.66.refs_0_), channel_id=1, source_target_pairs={{0,3},{1,2},{2,1},{3,0},{4,7},{5,6},{6,5},{7,4},{8,11},{9,10},{10,... | collective-permute-start | bytes 393224 | tf_op jit(solution)/shard_map/ppermute | solution.py:56
  42.9 8.0 %collective-permute-start.23 = (bf16[128,512]{1,0:T(8,128)(2,1)S(1)}, bf16[128,512]{1,0:T(8,128)(2,1)S(1)}, u32[]{:S(2)}, u32[]{:S(2)}) collective-permute-start(bf16[128,512]{1,0:T(8,128)(2,1)S(1)} %get-tuple-element.72), channel_id=1, source_target_pairs={{0,16},{4,20},{8,24},{12,28},{16,0},{20,4},{24,8},{28,12},{1,17},{... | collective-permute-start | bytes 393224 | tf_op jit(solution)/shard_map/ppermute | solution.py:497
  43.3 7.8 %collective-permute-start.20 = (bf16[64,512]{1,0:T(8,128)(2,1)S(1)}, bf16[64,512]{1,0:T(8,128)(2,1)S(1)}, u32[]{:S(2)}, u32[]{:S(2)}) collective-permute-start(bf16[64,512]{1,0:T(8,128)(2,1)S(1)} %get-tuple-element.69), channel_id=1, source_target_pairs={{0,4},{4,0},{8,12},{12,8},{16,20},{20,16},{24,28},{28,24},{1,5},{5... | collective-permute-start | bytes 196616 | tf_op jit(solution)/shard_map/ppermute | solution.py:56
  43.3 9.6 %collective-permute-start.21 = (bf16[64,512]{1,0:T(8,128)(2,1)S(1)}, bf16[64,512]{1,0:T(8,128)(2,1)S(1)}, u32[]{:S(2)}, u32[]{:S(2)}) collective-permute-start(bf16[64,512]{1,0:T(8,128)(2,1)S(1)} %get-tuple-element.70), channel_id=1, source_target_pairs={{0,8},{4,12},{8,0},{12,4},{16,24},{20,28},{24,16},{28,20},{1,9},{5... | collective-permute-start | bytes 196616 | tf_op jit(solution)/shard_map/ppermute | solution.py:56
  45.4 7.4 %collective-permute-start.22 = (bf16[64,512]{1,0:T(8,128)(2,1)S(1)}, bf16[64,512]{1,0:T(8,128)(2,1)S(1)}, u32[]{:S(2)}, u32[]{:S(2)}) collective-permute-start(bf16[64,512]{1,0:T(8,128)(2,1)S(1)} %get-tuple-element.71), channel_id=1, source_target_pairs={{0,12},{4,8},{8,4},{12,0},{16,28},{20,24},{24,20},{28,16},{1,13},{... | collective-permute-start | bytes 196616 | tf_op jit(solution)/shard_map/ppermute | solution.py:56
  50.9 2.2 %collective-permute-start.24 = (bf16[64,512]{1,0:T(8,128)(2,1)S(1)}, bf16[64,512]{1,0:T(8,128)(2,1)S(1)}, u32[]{:S(2)}, u32[]{:S(2)}) collective-permute-start(bf16[64,512]{1,0:T(8,128)(2,1)S(1)} %get-tuple-element.74), channel_id=1, source_target_pairs={{0,4},{4,0},{8,12},{12,8},{16,20},{20,16},{24,28},{28,24},{1,5},{5... | collective-permute-start | bytes 196616 | tf_op jit(solution)/shard_map/ppermute | solution.py:56
  51.0 5.0 %collective-permute-start.25 = (bf16[64,512]{1,0:T(8,128)(2,1)S(1)}, bf16[64,512]{1,0:T(8,128)(2,1)S(1)}, u32[]{:S(2)}, u32[]{:S(2)}) collective-permute-start(bf16[64,512]{1,0:T(8,128)(2,1)S(1)} %get-tuple-element.75), channel_id=1, source_target_pairs={{0,8},{4,12},{8,0},{12,4},{16,24},{20,28},{24,16},{28,20},{1,9},{5... | collective-permute-start | bytes 196616 | tf_op jit(solution)/shard_map/ppermute | solution.py:56
  51.1 5.3 %collective-permute-start.26 = (bf16[64,512]{1,0:T(8,128)(2,1)S(1)}, bf16[64,512]{1,0:T(8,128)(2,1)S(1)}, u32[]{:S(2)}, u32[]{:S(2)}) collective-permute-start(bf16[64,512]{1,0:T(8,128)(2,1)S(1)} %get-tuple-element.76), channel_id=1, source_target_pairs={{0,12},{4,8},{8,4},{12,0},{16,28},{20,24},{24,20},{28,16},{1,13},{... | collective-permute-start | bytes 196616 | tf_op jit(solution)/shard_map/ppermute | solution.py:56
